TPU v7x, 32 devices: a whole 2x2x4 slice. The times are simulated.
32 devices in a mesh: ctx: 2 (over core), dp: 16 (over z, y, x).
Axes of the slice: x: 2, y: 2, z: 4, core: 2. Of those that a mesh axis runs over, the one named last changes fastest.
Arguments:
- tokens: bfloat16 [16, 1024, 768], P('dp', 'ctx'), may hold values from -6 to 6
- lengths: int32 [16], P('dp'), may hold values from 256 to 1024, as said below
- qkv_weight: bfloat16 [768, 2304], P('dp'), may hold values from -0.21875 to 0.21875
- query_bias: bfloat16 [768], P('dp'), may hold values from -3 to 3
- value_bias: bfloat16 [768], P('dp'), may hold values from -0.1796875 to 0.1796875
- out_weight: bfloat16 [768, 768], P('dp'), may hold values from -4 to 4
- out_bias: bfloat16 [768], P('dp'), may hold values from -0.59765625 to 0.59765625
- norm1_gain: bfloat16 [768], P('dp'), may hold values from 0.5 to 1.5
- norm1_shift: bfloat16 [768], P('dp'), may hold values from -0.59765625 to 0.59765625
- up_weight: bfloat16 [768, 3072], P('dp'), may hold values from -0.21875 to 0.21875
- up_bias: bfloat16 [3072], P('dp'), may hold values from -3 to 3
- down_weight: bfloat16 [3072, 768], P('dp'), may hold values from -0.109375 to 0.109375
- down_bias: bfloat16 [768], P('dp'), may hold values from -0.59765625 to 0.59765625
- norm2_gain: bfloat16 [768], P('dp'), may hold values from 0.5 to 1.5
- norm2_shift: bfloat16 [768], P('dp'), may hold values from -0.59765625 to 0.59765625
- cotangent: bfloat16 [16, 1024, 768], P('dp', 'ctx'), may hold values from -6 to 6
Outputs:
- output: bfloat16 [16, 1024, 768], P('dp', 'ctx')
- input_grad: float32 [16, 1024, 768], P('dp', 'ctx')
- stream_rms: float32 [3], replicated
- grad_qkv_weight: float32 [768, 2304], P('dp')
- grad_query_bias: float32 [768], P('dp')
- grad_value_bias: float32 [768], P('dp')
- grad_out_weight: float32 [768, 768], P('dp')
- grad_out_bias: float32 [768], P('dp')
- grad_norm1_gain: float32 [768], P('dp')
- grad_norm1_shift: float32 [768], P('dp')
- grad_up_weight: float32 [768, 3072], P('dp')
- grad_up_bias: float32 [3072], P('dp')
- grad_down_weight: float32 [3072, 768], P('dp')
- grad_down_bias: float32 [768], P('dp')
- grad_norm2_gain: float32 [768], P('dp')
- grad_norm2_shift: float32 [768], P('dp')
Inputs may be any that keep to these rules, and one draw needn't show every extreme that they name: The first lengths[b] tokens of sequence b are real and the rest is padding; in every draw some sequence has 1024 valid tokens and some has 256.
All inputs are finite; a program needn't handle non-finite values.
Results may differ from a plain program's by a relative error of at most 0.02.
Values may be sent and summed in bfloat16 or wider, within the bound.
No kernel may reach another device: no remote copies, remote signals or barrier semaphores. Data moves between devices by JAX's collectives and lax.ppermute only.
A program may use at most 128 MiB of HBM per device.

v0:
```python
import math

import jax
import jax.numpy as jnp
from jax import lax
from jax.sharding import PartitionSpec as P

HEADS = 12


masked_score = -1e30
norm_eps = 1e-05


def layer_norm(resid, gain, shift):
    center = resid - jnp.mean(resid, axis=-1, keepdims=True)
    spread = jnp.mean(center * center, axis=-1, keepdims=True)
    return center * lax.rsqrt(spread + norm_eps) * gain + shift


def exact_gelu(upper_pre):
    return jax.nn.gelu(upper_pre, approximate=False)


def matmul(left, right):
    return jnp.dot(left, right, preferred_element_type=jnp.float32)


def inner_rows(left, right):
    return lax.dot_general(
        left, right, (((0,), (0,)), ((), ())), preferred_element_type=jnp.float32
    )


def outer_rows(left, right):
    return lax.dot_general(
        left, right, (((1,), (1,)), ((), ())), preferred_element_type=jnp.float32
    )


def head_slice(source, key_start, key_span, head_count):
    piece = lax.dynamic_slice_in_dim(source, key_start, key_span, 0)
    return piece.reshape(key_span, head_count, -1)


def block_scores(query, keys, key_start, key_span, length, score_scale):
    head_count = query.shape[1]
    key_block = head_slice(keys, key_start, key_span, head_count)
    raw_scores = (
        jnp.einsum("qhd,khd->hqk", query, key_block, preferred_element_type=jnp.float32)
        * score_scale
    )
    position = key_start + lax.iota(jnp.int32, key_span)
    return jnp.where((position < length)[None, None, :], raw_scores, masked_score)


def attend_forward(query, keys, values, length, key_span, score_scale):
    query_count, head_count, head_dim = query.shape
    block_count = (length + key_span - 1) // key_span

    def first_sweep(block_index, carry):
        running_max, running_sum = carry
        scores = block_scores(query, keys, block_index * key_span, key_span, length, score_scale)
        new_max = jnp.maximum(running_max, jnp.max(scores, axis=-1))
        running_sum = running_sum * jnp.exp(running_max - new_max) + jnp.sum(
            jnp.exp(scores - new_max[..., None]), axis=-1
        )
        return (new_max, running_sum)

    initial = (
        jnp.full((head_count, query_count), masked_score, jnp.float32),
        jnp.zeros((head_count, query_count), jnp.float32),
    )
    row_peak, row_total = lax.fori_loop(0, block_count, first_sweep, initial)
    log_total = row_peak + jnp.log(row_total)

    def second_sweep(block_index, accumulated):
        key_start = block_index * key_span
        scores = block_scores(query, keys, key_start, key_span, length, score_scale)
        weights = jnp.exp(scores - log_total[..., None]).astype(jnp.bfloat16)
        value_block = head_slice(values, key_start, key_span, head_count)
        return accumulated + jnp.einsum(
            "hqk,khd->qhd", weights, value_block, preferred_element_type=jnp.float32
        )

    mixed_heads = lax.fori_loop(
        0, block_count, second_sweep, jnp.zeros((query_count, head_count, head_dim), jnp.float32)
    )
    return (mixed_heads, log_total)


def attend_backward(
    query, keys, values, grad_mixed, mixed_heads, log_total, length, key_span, score_scale
):
    query_count, head_count, head_dim = query.shape
    seq_len = keys.shape[0]
    block_count = (length + key_span - 1) // key_span
    row_delta = jnp.transpose(jnp.sum(grad_mixed.astype(jnp.float32) * mixed_heads, axis=-1))

    def grad_sweep(block_index, carry):
        grad_query, grad_keys, grad_values = carry
        key_start = block_index * key_span
        scores = block_scores(query, keys, key_start, key_span, length, score_scale)
        block_probs = jnp.exp(scores - log_total[..., None])
        value_block = head_slice(values, key_start, key_span, head_count)
        grad_probs = jnp.einsum(
            "qhd,khd->hqk", grad_mixed, value_block, preferred_element_type=jnp.float32
        )
        grad_scores = (block_probs * (grad_probs - row_delta[..., None])).astype(jnp.bfloat16)
        key_block = head_slice(keys, key_start, key_span, head_count)
        grad_query = grad_query + score_scale * jnp.einsum(
            "hqk,khd->qhd", grad_scores, key_block, preferred_element_type=jnp.float32
        )
        key_part = score_scale * jnp.einsum(
            "hqk,qhd->khd", grad_scores, query, preferred_element_type=jnp.float32
        )
        value_part = jnp.einsum(
            "hqk,qhd->khd",
            block_probs.astype(jnp.bfloat16),
            grad_mixed,
            preferred_element_type=jnp.float32,
        )
        grad_keys = lax.dynamic_update_slice_in_dim(
            grad_keys, key_part.reshape(key_span, head_count * head_dim), key_start, 0
        )
        grad_values = lax.dynamic_update_slice_in_dim(
            grad_values, value_part.reshape(key_span, head_count * head_dim), key_start, 0
        )
        return (grad_query, grad_keys, grad_values)

    initial = (
        jnp.zeros((query_count, head_count, head_dim), jnp.float32),
        jnp.zeros((seq_len, head_count * head_dim), jnp.float32),
        jnp.zeros((seq_len, head_count * head_dim), jnp.float32),
    )
    grad_query, grad_keys, grad_values = lax.fori_loop(0, block_count, grad_sweep, initial)
    return (grad_query.reshape(query_count, head_count * head_dim), grad_keys, grad_values)


def shards(
    tokens,
    lengths,
    qkv_weight,
    query_bias,
    value_bias,
    out_weight,
    out_bias,
    norm1_gain,
    norm1_shift,
    up_weight,
    up_bias,
    down_weight,
    down_bias,
    norm2_gain,
    norm2_shift,
    cotangent,
):
    seq_dev, ctx_tok, model_width = tokens.shape
    head_dim = model_width // HEADS
    score_scale = head_dim ** (-0.5)
    seq_len = ctx_tok * lax.axis_size("ctx")
    key_span = math.gcd(seq_len, 512)
    total_rows = seq_dev * ctx_tok
    positions = lax.axis_index("ctx") * ctx_tok + lax.iota(jnp.int32, ctx_tok)
    valid_rows = (positions[None, :] < lengths[:, None]).reshape(total_rows, 1)
    rows_in = tokens.reshape(total_rows, model_width)
    attn_set = (
        lax.all_gather(qkv_weight, "dp", axis=0, tiled=True),
        lax.all_gather(query_bias, "dp", axis=0, tiled=True),
        lax.all_gather(value_bias, "dp", axis=0, tiled=True),
        lax.all_gather(out_weight, "dp", axis=0, tiled=True),
        lax.all_gather(out_bias, "dp", axis=0, tiled=True),
        lax.all_gather(norm1_gain, "dp", axis=0, tiled=True),
        lax.all_gather(norm1_shift, "dp", axis=0, tiled=True),
    )
    ffn_set = (
        lax.all_gather(up_weight, "dp", axis=0, tiled=True),
        lax.all_gather(up_bias, "dp", axis=0, tiled=True),
        lax.all_gather(down_weight, "dp", axis=0, tiled=True),
        lax.all_gather(down_bias, "dp", axis=0, tiled=True),
        lax.all_gather(norm2_gain, "dp", axis=0, tiled=True),
        lax.all_gather(norm2_shift, "dp", axis=0, tiled=True),
    )
    projected = matmul(rows_in, attn_set[0])
    query_rows = (projected[:, :model_width] + attn_set[1].astype(jnp.float32)).astype(jnp.bfloat16)
    key_rows = projected[:, model_width : 2 * model_width].astype(jnp.bfloat16)
    value_rows = (projected[:, 2 * model_width :] + attn_set[2].astype(jnp.float32)).astype(
        jnp.bfloat16
    )
    key_local = key_rows.reshape(seq_dev, ctx_tok, model_width)
    value_local = value_rows.reshape(seq_dev, ctx_tok, model_width)
    key_seq, value_seq = (
        lax.all_gather(key_local, "ctx", axis=1, tiled=True),
        lax.all_gather(value_local, "ctx", axis=1, tiled=True),
    )
    query_seq = query_rows.reshape(seq_dev, ctx_tok, HEADS, head_dim)
    member = 0
    mixed_heads, log_total = attend_forward(
        query_seq[member],
        key_seq[member],
        value_seq[member],
        lengths[member],
        key_span,
        score_scale,
    )
    head_parts = [mixed_heads]
    mixed_parts = mixed_heads.reshape(ctx_tok, model_width)
    log_parts = [log_total]
    mixed_rows = mixed_parts.astype(jnp.bfloat16)
    attn_branch = matmul(mixed_rows, attn_set[3]) + attn_set[4].astype(jnp.float32)
    input_float = rows_in.astype(jnp.float32)
    resid1 = input_float + attn_branch
    hidden1 = layer_norm(resid1, attn_set[5].astype(jnp.float32), attn_set[6].astype(jnp.float32))
    hidden_low = hidden1.astype(jnp.bfloat16)
    upper_pre = matmul(hidden_low, ffn_set[0]) + ffn_set[1].astype(jnp.float32)
    activated = exact_gelu(upper_pre).astype(jnp.bfloat16)
    ffn_branch = matmul(activated, ffn_set[2]) + ffn_set[3].astype(jnp.float32)
    resid2 = hidden1 + ffn_branch
    output = layer_norm(
        resid2, ffn_set[4].astype(jnp.float32), ffn_set[5].astype(jnp.float32)
    ).astype(jnp.bfloat16)
    totals = lax.psum(
        (
            jnp.sum(jnp.where(valid_rows, input_float * input_float, 0.0)),
            jnp.sum(jnp.where(valid_rows, attn_branch * attn_branch, 0.0)),
            jnp.sum(jnp.where(valid_rows, ffn_branch * ffn_branch, 0.0)),
            jnp.sum(valid_rows.astype(jnp.float32)),
        ),
        ("ctx", "dp"),
    )
    stream_rms = jnp.sqrt(
        jnp.stack([totals[0], totals[1], totals[2]]) / (totals[3] * model_width) + 1e-06
    )
    renewed = lax.optimization_barrier(
        (
            qkv_weight,
            query_bias,
            value_bias,
            out_weight,
            out_bias,
            norm1_gain,
            norm1_shift,
            up_weight,
            up_bias,
            down_weight,
            down_bias,
            norm2_gain,
            norm2_shift,
            cotangent,
        )
    )
    back_attn = (
        lax.all_gather(renewed[0], "dp", axis=0, tiled=True),
        lax.all_gather(renewed[1], "dp", axis=0, tiled=True),
        lax.all_gather(renewed[2], "dp", axis=0, tiled=True),
        lax.all_gather(renewed[3], "dp", axis=0, tiled=True),
        lax.all_gather(renewed[4], "dp", axis=0, tiled=True),
        lax.all_gather(renewed[5], "dp", axis=0, tiled=True),
        lax.all_gather(renewed[6], "dp", axis=0, tiled=True),
    )
    back_ffn = (
        lax.all_gather(renewed[7], "dp", axis=0, tiled=True),
        lax.all_gather(renewed[8], "dp", axis=0, tiled=True),
        lax.all_gather(renewed[9], "dp", axis=0, tiled=True),
        lax.all_gather(renewed[10], "dp", axis=0, tiled=True),
        lax.all_gather(renewed[11], "dp", axis=0, tiled=True),
        lax.all_gather(renewed[12], "dp", axis=0, tiled=True),
    )
    grad_rows = cotangent.reshape(total_rows, model_width).astype(jnp.float32)
    _, norm2_back = jax.vjp(
        layer_norm, resid2, back_ffn[4].astype(jnp.float32), back_ffn[5].astype(jnp.float32)
    )
    grad_resid2, grad_gain2, grad_shift2 = norm2_back(grad_rows)
    grad_ffn = grad_resid2.astype(jnp.bfloat16)
    grad_down = inner_rows(activated, grad_ffn)
    grad_down_bias = jnp.sum(grad_ffn, axis=0, dtype=jnp.float32)
    _, gelu_back = jax.vjp(exact_gelu, upper_pre)
    grad_upper = gelu_back(outer_rows(grad_ffn, back_ffn[2]))[0].astype(jnp.bfloat16)
    grad_up = inner_rows(hidden_low, grad_upper)
    grad_up_bias = jnp.sum(grad_upper, axis=0, dtype=jnp.float32)
    grad_hidden1 = grad_resid2 + outer_rows(grad_upper, back_ffn[0])
    ffn_grads = (
        lax.psum_scatter(
            grad_up.astype(jnp.bfloat16), "dp", scatter_dimension=0, tiled=True
        ).astype(jnp.float32),
        lax.psum_scatter(
            grad_up_bias.astype(jnp.bfloat16), "dp", scatter_dimension=0, tiled=True
        ).astype(jnp.float32),
        lax.psum_scatter(
            grad_down.astype(jnp.bfloat16), "dp", scatter_dimension=0, tiled=True
        ).astype(jnp.float32),
        lax.psum_scatter(
            grad_down_bias.astype(jnp.bfloat16), "dp", scatter_dimension=0, tiled=True
        ).astype(jnp.float32),
        lax.psum_scatter(
            grad_gain2.astype(jnp.bfloat16), "dp", scatter_dimension=0, tiled=True
        ).astype(jnp.float32),
        lax.psum_scatter(
            grad_shift2.astype(jnp.bfloat16), "dp", scatter_dimension=0, tiled=True
        ).astype(jnp.float32),
    )
    _, norm1_back = jax.vjp(
        layer_norm, resid1, back_attn[5].astype(jnp.float32), back_attn[6].astype(jnp.float32)
    )
    grad_resid1, grad_gain1, grad_shift1 = norm1_back(grad_hidden1)
    grad_attn = grad_resid1.astype(jnp.bfloat16)
    grad_out = inner_rows(mixed_rows, grad_attn)
    grad_out_bias = jnp.sum(grad_attn, axis=0, dtype=jnp.float32)
    grad_mixed = (
        outer_rows(grad_attn, back_attn[3])
        .astype(jnp.bfloat16)
        .reshape(seq_dev, ctx_tok, HEADS, head_dim)
    )
    back_keys, back_values = (key_seq, value_seq)
    member = 0
    grad_query, grad_keys, grad_values = attend_backward(
        query_seq[member],
        back_keys[member],
        back_values[member],
        grad_mixed[member],
        head_parts[member],
        log_parts[member],
        lengths[member],
        key_span,
        score_scale,
    )
    key_share = lax.psum_scatter(
        grad_keys.astype(jnp.bfloat16), "ctx", scatter_dimension=0, tiled=True
    )
    value_share = lax.psum_scatter(
        grad_values.astype(jnp.bfloat16), "ctx", scatter_dimension=0, tiled=True
    )
    query_grads = grad_query.astype(jnp.bfloat16)
    grad_qkv_rows = jnp.concatenate([query_grads, key_share, value_share], axis=1)
    grad_qkv = inner_rows(rows_in, grad_qkv_rows)
    grad_query_bias = jnp.sum(grad_qkv_rows[:, :model_width], axis=0, dtype=jnp.float32)
    grad_value_bias = jnp.sum(grad_qkv_rows[:, 2 * model_width :], axis=0, dtype=jnp.float32)
    input_grad = grad_resid1 + outer_rows(grad_qkv_rows, back_attn[0])
    attn_grads = (
        lax.psum_scatter(
            grad_qkv.astype(jnp.bfloat16), "dp", scatter_dimension=0, tiled=True
        ).astype(jnp.float32),
        lax.psum_scatter(
            grad_query_bias.astype(jnp.bfloat16), "dp", scatter_dimension=0, tiled=True
        ).astype(jnp.float32),
        lax.psum_scatter(
            grad_value_bias.astype(jnp.bfloat16), "dp", scatter_dimension=0, tiled=True
        ).astype(jnp.float32),
        lax.psum_scatter(
            grad_out.astype(jnp.bfloat16), "dp", scatter_dimension=0, tiled=True
        ).astype(jnp.float32),
        lax.psum_scatter(
            grad_out_bias.astype(jnp.bfloat16), "dp", scatter_dimension=0, tiled=True
        ).astype(jnp.float32),
        lax.psum_scatter(
            grad_gain1.astype(jnp.bfloat16), "dp", scatter_dimension=0, tiled=True
        ).astype(jnp.float32),
        lax.psum_scatter(
            grad_shift1.astype(jnp.bfloat16), "dp", scatter_dimension=0, tiled=True
        ).astype(jnp.float32),
    )
    summed = (
        lax.psum(attn_grads[0].astype(jnp.bfloat16), "ctx").astype(jnp.float32),
        lax.psum(attn_grads[1].astype(jnp.bfloat16), "ctx").astype(jnp.float32),
        lax.psum(attn_grads[2].astype(jnp.bfloat16), "ctx").astype(jnp.float32),
        lax.psum(attn_grads[3].astype(jnp.bfloat16), "ctx").astype(jnp.float32),
        lax.psum(attn_grads[4].astype(jnp.bfloat16), "ctx").astype(jnp.float32),
        lax.psum(attn_grads[5].astype(jnp.bfloat16), "ctx").astype(jnp.float32),
        lax.psum(attn_grads[6].astype(jnp.bfloat16), "ctx").astype(jnp.float32),
        lax.psum(ffn_grads[0].astype(jnp.bfloat16), "ctx").astype(jnp.float32),
        lax.psum(ffn_grads[1].astype(jnp.bfloat16), "ctx").astype(jnp.float32),
        lax.psum(ffn_grads[2].astype(jnp.bfloat16), "ctx").astype(jnp.float32),
        lax.psum(ffn_grads[3].astype(jnp.bfloat16), "ctx").astype(jnp.float32),
        lax.psum(ffn_grads[4].astype(jnp.bfloat16), "ctx").astype(jnp.float32),
        lax.psum(ffn_grads[5].astype(jnp.bfloat16), "ctx").astype(jnp.float32),
    )
    return (
        output.reshape(seq_dev, ctx_tok, model_width),
        input_grad.reshape(seq_dev, ctx_tok, model_width),
        stream_rms,
        summed[0],
        summed[1],
        summed[2],
        summed[3],
        summed[4],
        summed[5],
        summed[6],
        summed[7],
        summed[8],
        summed[9],
        summed[10],
        summed[11],
        summed[12],
    )


def solution(mesh):
    in_specs = (
        P("dp", "ctx", None),
        P("dp"),
        P("dp", None),
        P("dp"),
        P("dp"),
        P("dp", None),
        P("dp"),
        P("dp"),
        P("dp"),
        P("dp", None),
        P("dp"),
        P("dp", None),
        P("dp"),
        P("dp"),
        P("dp"),
        P("dp", "ctx", None),
    )
    out_specs = (
        P("dp", "ctx", None),
        P("dp", "ctx", None),
        P(),
        P("dp", None),
        P("dp"),
        P("dp"),
        P("dp", None),
        P("dp"),
        P("dp"),
        P("dp"),
        P("dp", None),
        P("dp"),
        P("dp", None),
        P("dp"),
        P("dp"),
        P("dp"),
    )
    return jax.shard_map(shards, mesh=mesh, in_specs=in_specs, out_specs=out_specs, check_vma=False)
```

profile of v0, /device:TPU:0, one launch (start us, length us, event | category | flops | bytes accessed | tf_op | source)
XLA Modules:
  0.0 1374.7 jit_solution(11127994549599021037)
XLA Ops:
  8.1 76.7 %all-gather.13.cloned.1.call-done = bf16[768,2304]{1,0:T(8,128)(2,1)} async-done(((bf16[48,2304]{1,0:T(8,128)(2,1)}), bf16[768,2304]{1,0:T(8,128)(2,1)}) %all-gather.13.cloned.1.call-update) | async-done | bytes 3538960 | tf_op jit(solution)/shard_map/all_gather | solution.py:168
  96.3 74.4 %all-reduce.22 = (bf16[768]{0:T(1024)(128)(2,1)S(1)}, bf16[768]{0:T(1024)(128)(2,1)S(1)}, bf16[768]{0:T(1024)(128)(2,1)S(1)}, bf16[768]{0:T(1024)(128)(2,1)S(1)}...) all-reduce(bf16[768]{0:T(1024)(128)(2,1)S(1)} %dynamic-update-slice, ...), channel_id=1, replica_groups=mesh['ctx'=2,'dp'=16] {'dp'}, use_global_device_ids=true, to_apply=%add.1 | all-reduce | flops 9216 | bytes 36864
  181.2 13.2 while.36
  198.4 21.6 %while.37 = (s32[]{:T(128)}, f32[512,12,64]{0,2,1:T(8,128)}, s32[]{:T(128)}, bf16[1024,768]{0,1:T(8,128)(2,1)}, s32[]{:T(128)}, /*index=5*/bf16[1024,768]{0,1:T(...) while((s32[]{:T(128)}, f32[512,12,64]{0,2,1:T(8,128)}, ...), condition=%wide.region_5.6_spmd, body=%wide.region_4.5_spmd.sunk | while | flops 818283520 | bytes 8676527 | solution.py:86
  212.1 7.5 bitcast_add_fusion.4
  222.4 17.1 %all-gather.15.cloned.1.call-done = bf16[768,768]{1,0:T(8,128)(2,1)} async-done(((bf16[48,768]{1,0:T(8,128)(2,1)}), bf16[768,768]{1,0:T(8,128)(2,1)}) %all-gather.15.cloned.1.call-update) | async-done | bytes 1179664 | tf_op jit(solution)/shard_map/all_gather | solution.py:171
  244.7 76.8 %all-gather.17.cloned.1.call-done = bf16[768,3072]{1,0:T(8,128)(2,1)} async-done(((bf16[48,3072]{1,0:T(8,128)(2,1)}), bf16[768,3072]{1,0:T(8,128)(2,1)}) %all-gather.17.cloned.1.call-update) | async-done | bytes 4718608 | tf_op jit(solution)/shard_map/all_gather | solution.py:177
  321.5 20.8 %multiply_convert_fusion.1 = (bf16[512,3072]{1,0:T(8,128)(2,1)}, f32[512,3072]{1,0:T(8,128)}, f32[512,3072]{1,0:T(8,128)}) fusion(f32[3072]{0:T(1024)S(1)} %convert_element_type.216, bf16[768,3072]{1,0:T(8,128)(2,1)} %all-gather.17.cloned.1.call-done, f32[512,768]{1,0:T(8,128)} %copy-done.6, f32[768]{0:T(1024)S(1)} %convert_element_type.214, ...), kind=kOutput, calls=%fused_computation.35 | convolution fusion | flops 2521694208 | bytes 22042624 | tf_op jit(solution)/shard_map/dot_general | solution.py:26
  342.3 61.0 %all-gather.19.cloned.1.call-done = bf16[3072,768]{1,0:T(8,128)(2,1)} async-done(((bf16[192,768]{1,0:T(8,128)(2,1)}), bf16[3072,768]{1,0:T(8,128)(2,1)}) %all-gather.19.cloned.1.call-update) | async-done | bytes 4718608 | tf_op jit(solution)/shard_map/all_gather | solution.py:179
  403.3 8.3 fusion.25
  416.7 68.3 %all-gather.21.cloned.1.call-done = bf16[3072,768]{1,0:T(8,128)(2,1)} async-done(((bf16[192,768]{1,0:T(8,128)(2,1)}), bf16[3072,768]{1,0:T(8,128)(2,1)}) %all-gather.21.cloned.1.call-update) | async-done | bytes 4718608 | tf_op jit(solution)/shard_map/all_gather | solution.py:264
  485.0 12.9 fusion.42
  497.9 69.0 %all-gather.23.cloned.1.call-done = bf16[768,3072]{1,0:T(8,128)(2,1)} async-done(((bf16[48,3072]{1,0:T(8,128)(2,1)}), bf16[768,3072]{1,0:T(8,128)(2,1)}) %all-gather.23.cloned.1.call-update) | async-done | bytes 4718608 | tf_op jit(solution)/shard_map/all_gather | solution.py:262
  566.9 8.0 multiply_reduce_fusion
  578.3 46.1 %all-gather.25.cloned.1.call-done = bf16[768,768]{1,0:T(8,128)(2,1)} async-done(((bf16[48,768]{1,0:T(8,128)(2,1)}), bf16[768,768]{1,0:T(8,128)(2,1)}) %all-gather.25.cloned.1.call-update) | async-done | bytes 1179664 | tf_op jit(solution)/shard_map/all_gather | solution.py:256
  636.2 53.6 %while.38 = (s32[]{:T(128)}, f32[512,12,64]{0,2,1:T(8,128)}, bf16[1024,768]{0,1:T(8,128)(2,1)}, bf16[1024,768]{0,1:T(8,128)(2,1)}, s32[]{:T(128)}, /*index=5*/bf...) while((s32[]{:T(128)}, f32[512,12,64]{0,2,1:T(8,128)}, ...), condition=%wide.region_16.17_spmd, body=%wide.region_15.16_spmd.sunk | while | flops 2046297088 | bytes 117253952 | solution.py:136
  697.9 12.6 reduce-scatter.9.cloned.1.call-done
  738.9 41.5 %all-reduce.20 = (f32[1]{0:T(128)}, f32[1]{0:T(128)}, f32[1]{0:T(128)}, f32[]{:T(128)}) all-reduce(f32[1]{0:T(128)} %bitcast.26, f32[1]{0:T(128)} %bitcast.25, f32[1]{0:T(128)} %bitcast.24, f32[]{:T(128)} %get-tuple-element.409), channel_id=1, replica_groups=mesh['ctx'=2,'dp'=16] {'ctx','dp'}, use_global_device_ids=true, to_apply=%region_24.25 | all-reduce | flops 4 | bytes 32 | tf_op jit(solution)/shard_map/psum | solution.py:222
  785.1 76.4 %all-reduce.21 = (bf16[768]{0:T(1024)(128)(2,1)S(1)}, bf16[768]{0:T(1024)(128)(2,1)S(1)}, bf16[768]{0:T(1024)(128)(2,1)S(1)}, bf16[768]{0:T(1024)(128)(2,1)S(1)}...) all-reduce(bf16[768]{0:T(1024)(128)(2,1)S(1)} %dynamic-update-slice, ...), channel_id=1, replica_groups=mesh['ctx'=2,'dp'=16] {'dp'}, use_global_device_ids=true, to_apply=%add.8 | all-reduce | flops 10752 | bytes 43008
  871.5 110.8 %reduce-scatter.13.cloned.1.call-done = bf16[48,768]{1,0:T(8,128)(2,1)} async-done(((bf16[768,768]{1,0:T(8,128)(2,1)}), bf16[48,768]{1,0:T(8,128)(2,1)}) %reduce-scatter.13.cloned.1.call-update) | async-done | bytes 73744 | tf_op jit(solution)/shard_map/reduce_scatter | solution.py:349
  982.3 141.6 %reduce-scatter.17.cloned.1.call-done = bf16[192,768]{1,0:T(8,128)(2,1)} async-done(((bf16[3072,768]{1,0:T(8,128)(2,1)}), bf16[192,768]{1,0:T(8,128)(2,1)}) %reduce-scatter.17.cloned.1.call-update) | async-done | bytes 294928 | tf_op jit(solution)/shard_map/reduce_scatter | solution.py:289
  1123.9 142.1 %reduce-scatter.15.cloned.1.call-done = bf16[48,3072]{1,0:T(8,128)(2,1)} async-done(((bf16[768,3072]{1,0:T(8,128)(2,1)}), bf16[48,3072]{1,0:T(8,128)(2,1)}) %reduce-scatter.15.cloned.1.call-update) | async-done | bytes 294928 | tf_op jit(solution)/shard_map/reduce_scatter | solution.py:283
  1267.3 71.7 %all-gather.27.cloned.1.call-done = bf16[768,2304]{1,0:T(8,128)(2,1)} async-done(((bf16[48,2304]{1,0:T(8,128)(2,1)}), bf16[768,2304]{1,0:T(8,128)(2,1)}) %all-gather.27.cloned.1.call-update) | async-done | bytes 3538960 | tf_op jit(solution)/shard_map/all_gather | solution.py:253
  1344.9 15.7 %all-reduce.27.cloned.1.call-done = (bf16[48,2304]{0,1:T(8,128)(2,1)}, bf16[48,768]{1,0:T(8,128)(2,1)}, bf16[48,3072]{1,0:T(8,128)(2,1)}, bf16[192,768]{1,0:T(8,128)(2,1)}) async-done(((bf16[48,2304]{0,1:T(8,128)(2,1)}, bf16[48,768]{1,0:T(8,128)(2,1)}, bf16[48,3072]{1,0:T(8,128)(2,1)}, bf16[192,768]{1,0:T(8,128)(2,1)}), (bf16[48,2304]{0,1:T(8,128)(2,1)}, bf16[48,768]{1,0:T(8,128)(2,1)}, ...) | async-done | bytes 884752 | tf_op jit(solution)/shard_map/psum | solution.py:363
  (273 shorter events, 195.6 us)
Async XLA Ops:
  7.2 77.6 %all-gather.13.cloned.1.call-start = ((), (), s32[]{:S(2)}) async-start(), calls=%async_computation.6 | async-start | bytes 3760128 | tf_op jit(solution)/shard_map/all_gather | solution.py:168
  8.0 88.0 %copy-start.39 = (bf16[192]{0:T(256)(128)(2,1)S(1)}, bf16[192]{0:T(256)(128)(2,1)}, u32[]{:S(2)}) copy-start(bf16[192]{0:T(256)(128)(2,1)} %param.32) | copy-start | bytes 1156
  8.0 171.4 %all-gather.31.cloned.1.call-start = ((), (), s32[]{:S(2)}) async-start(), calls=%async_computation.20 | async-start | bytes 2359296 | tf_op jit(solution)/shard_map/all_gather | solution.py:193
  92.1 102.3 %all-gather.29.cloned.1.call-start = ((), (), s32[]{:S(2)}) async-start(), calls=%async_computation.19 | async-start | bytes 2359296 | tf_op jit(solution)/shard_map/all_gather | solution.py:194
  173.7 65.8 %all-gather.15.cloned.1.call-start = ((), (), s32[]{:S(2)}) async-start(), calls=%async_computation.7 | async-start | bytes 1253376 | tf_op jit(solution)/shard_map/all_gather | solution.py:171
  174.3 147.3 %all-gather.17.cloned.1.call-start = ((), (), s32[]{:S(2)}) async-start(), calls=%async_computation.8 | async-start | bytes 5013504 | tf_op jit(solution)/shard_map/all_gather | solution.py:177
  174.9 228.5 %all-gather.19.cloned.1.call-start = ((), (), s32[]{:S(2)}) async-start(), calls=%async_computation.9 | async-start | bytes 5013504 | tf_op jit(solution)/shard_map/all_gather | solution.py:179
  175.4 309.6 %all-gather.21.cloned.1.call-start = ((), (), s32[]{:S(2)}) async-start(), calls=%async_computation.10 | async-start | bytes 5013504 | tf_op jit(solution)/shard_map/all_gather | solution.py:264
  176.2 390.7 %all-gather.23.cloned.1.call-start = ((), (), s32[]{:S(2)}) async-start(), calls=%async_computation.11 | async-start | bytes 5013504 | tf_op jit(solution)/shard_map/all_gather | solution.py:262
  176.9 447.6 %all-gather.25.cloned.1.call-start = ((), (), s32[]{:S(2)}) async-start(), calls=%async_computation.12 | async-start | bytes 1253376 | tf_op jit(solution)/shard_map/all_gather | solution.py:256
  177.7 520.2 %reduce-scatter.11.cloned.1.call-start = ((), (), s32[]{:S(2)}) async-start(), calls=%async_computation.14 | async-start | bytes 2359296 | tf_op jit(solution)/shard_map/reduce_scatter | solution.py:330
  178.4 224.9 %copy-start.26 = (f32[768]{0:T(1024)}, f32[768]{0:T(1024)S(1)}, u32[]{:S(2)}) copy-start(f32[768]{0:T(1024)S(1)} %convert_element_type.213) | copy-start | bytes 9220
  178.4 224.9 %copy-start.28 = (f32[768]{0:T(1024)}, f32[768]{0:T(1024)S(1)}, u32[]{:S(2)}) copy-start(f32[768]{0:T(1024)S(1)} %convert_element_type.214) | copy-start | bytes 9220
  689.8 20.7 %reduce-scatter.9.cloned.1.call-start = ((), (), s32[]{:S(2)}) async-start(), calls=%async_computation.13 | async-start | bytes 2359296 | tf_op jit(solution)/shard_map/reduce_scatter | solution.py:327
  690.5 179.0 %reduce-scatter.19.cloned.1.call-start = ((), (), s32[]{:S(2)}) async-start(), calls=%async_computation.21 | async-start | bytes 3760128
  718.3 264.0 %reduce-scatter.13.cloned.1.call-start = ((), (), s32[]{:S(2)}) async-start(), calls=%async_computation.16 | async-start | bytes 1253376 | tf_op jit(solution)/shard_map/reduce_scatter | solution.py:349
  721.5 402.4 %reduce-scatter.17.cloned.1.call-start = ((), (), s32[]{:S(2)}) async-start(), calls=%async_computation.18 | async-start | bytes 5013504 | tf_op jit(solution)/shard_map/reduce_scatter | solution.py:289
  728.2 537.8 %reduce-scatter.15.cloned.1.call-start = ((), (), s32[]{:S(2)}) async-start(), calls=%async_computation.17 | async-start | bytes 5013504 | tf_op jit(solution)/shard_map/reduce_scatter | solution.py:283
  736.2 529.8 %copy-start.5 = (f32[512,768]{1,0:T(8,128)S(1)}, f32[512,768]{1,0:T(8,128)}, u32[]{:S(2)}) copy-start(f32[512,768]{1,0:T(8,128)} %copy-done.4) | copy-start | bytes 4718596
  736.2 529.8 %copy-start.19 = (f32[512]{0:T(512)S(1)}, f32[512]{0:T(512)}, u32[]{:S(2)}) copy-start(f32[512]{0:T(512)} %copy-done.18) | copy-start | bytes 6148
  736.2 529.8 %copy-start.21 = (f32[512]{0:T(512)S(1)}, f32[512]{0:T(512)}, u32[]{:S(2)}) copy-start(f32[512]{0:T(512)} %copy-done.20) | copy-start | bytes 6148
  736.3 602.7 %all-gather.27.cloned.1.call-start = ((), (), s32[]{:S(2)}) async-start(), calls=%async_computation.15 | async-start | bytes 3760128 | tf_op jit(solution)/shard_map/all_gather | solution.py:253
  736.8 623.8 %all-reduce.27.cloned.1.call-start = ((), (), s32[]{:S(2)}) async-start(), calls=%async_computation.22 | async-start | bytes 2506752 | tf_op jit(solution)/shard_map/psum | solution.py:363
  737.5 601.5 %copy-start.13 = (f32[512,768]{1,0:T(8,128)S(1)}, f32[512,768]{1,0:T(8,128)}, u32[]{:S(2)}) copy-start(f32[512,768]{1,0:T(8,128)} %copy-done.12) | copy-start | bytes 4718596
  (40 other events, 1046.9 us)
Sparse Core Ops, SparseCore 0:
  10.8 73.9 all-gather.12
  92.3 8.3 all-gather.30
  173.8 5.6 all-gather.28
  182.2 57.2 all-gather.14
  242.1 79.3 all-gather.16
  324.2 79.0 all-gather.18
  406.1 78.8 all-gather.20
  487.8 79.0 all-gather.22
  569.7 54.7 all-gather.24
  689.9 7.9 reduce-scatter.10
  700.2 10.2 reduce-scatter.8
  718.4 135.6 reduce-scatter.18
  859.5 122.7 reduce-scatter.12
  987.3 136.5 reduce-scatter.16
  1129.7 136.2 reduce-scatter.14
  1268.7 70.2 all-gather.26
  1342.0 18.5 all-reduce.26
where the time goes:
time: 1380 us; the launch traced here: 1370 us
  waiting for transfers between devices  920 us (67%)
  blocking collectives  195 us (14%)
  matrix products  149 us (11%)
  local copies, waits for them, and re-layouts  48.5 us (4%)
  other arithmetic  41.1 us (3%)
  between operations  18.9 us (1%)
    unnamed x2, blocking collectives  151 us
    reduce_scatter x1, waiting for transfers between devices, shards(): lax.psum_scatter(grad_up.astype(jnp.bfloat16), 'dp', scatter_dimension=0,...  142 us
    reduce_scatter x1, waiting for transfers between devices, shards(): lax.psum_scatter(grad_down.astype(jnp.bfloat16), 'dp', scatter_dimension=...  142 us
    reduce_scatter x1, waiting for transfers between devices, shards(): lax.psum_scatter(grad_out.astype(jnp.bfloat16), 'dp', scatter_dimension=0...  111 us
    all_gather x1, waiting for transfers between devices, shards(): lax.all_gather(up_weight, 'dp', axis=0, tiled=True)  76.8 us
    all_gather x1, waiting for transfers between devices, shards(): lax.all_gather(qkv_weight, 'dp', axis=0, tiled=True)  76.7 us
    all_gather x1, waiting for transfers between devices, shards(): lax.all_gather(renewed[0], 'dp', axis=0, tiled=True)  71.7 us
    all_gather x1, waiting for transfers between devices, shards(): lax.all_gather(renewed[7], 'dp', axis=0, tiled=True)  69 us
  transfers between devices with their start and end apart: 17, of which 14 were waited for; matrix products, arithmetic and copies ran while one was open for 11% of the time, Pallas kernels for 0%

commit v1 on v0

--- a/solution.py
+++ b/solution.py
@@ -3,6 +3,8 @@
 import jax
 import jax.numpy as jnp
 from jax import lax
+from jax.experimental import pallas as pl
+from jax.experimental.pallas import tpu as pltpu
 from jax.sharding import PartitionSpec as P
 
 HEADS = 12
@@ -135,6 +137,223 @@
     )
     grad_query, grad_keys, grad_values = lax.fori_loop(0, block_count, grad_sweep, initial)
     return (grad_query.reshape(query_count, head_count * head_dim), grad_keys, grad_values)
+
+
+def low_precision(value):
+    return lax.reduce_precision(value, exponent_bits=8, mantissa_bits=7)
+
+
+class Links:
+    def __init__(self):
+        self.dp = lax.axis_size("dp")
+        self.ctx = lax.axis_size("ctx")
+        self.bits = self.dp.bit_length() - 1
+        assert self.dp == 1 << self.bits and self.bits >= 2 and self.ctx % 2 == 0
+        self.core = lax.axis_index("ctx") % 2
+        self.me = lax.axis_index("dp")
+        self.upper = []
+        bit = 2
+        while bit < self.bits:
+            self.upper.append((bit, min(2, self.bits - bit)))
+            bit += 2
+
+    def swap(self, value):
+        return lax.ppermute(value, "ctx", [(i, i ^ 1) for i in range(self.ctx)])
+
+    def hop(self, value, mask_even, mask_odd):
+        pairs = []
+        for block in range(self.ctx):
+            mask = mask_odd if block % 2 else mask_even
+            pairs += [(block * self.dp + i, block * self.dp + (i ^ mask)) for i in range(self.dp)]
+        return lax.ppermute(value, ("ctx", "dp"), pairs)
+
+    def places(self, core):
+        position = lax.iota(jnp.int32, self.dp)
+        quarter = self.dp // 4
+        first = (position // quarter) % 2
+        second = position // (2 * quarter)
+        mask = (position % quarter) * 4 + first * (1 + core) + second * (2 - core)
+        return jnp.bitwise_xor(self.me, mask)
+
+    def gather(self, piece):
+        held = piece
+        for bit, size in self.upper:
+            held = jnp.concatenate(
+                [held] + [self.hop(held, k << bit, k << bit) for k in range(1, 1 << size)], axis=0
+            )
+        held = jnp.concatenate([held, self.hop(held, 1, 2)], axis=0)
+        return jnp.concatenate([held, self.hop(held, 2, 1)], axis=0)
+
+    def reduce(self, kept, received):
+        rows = kept.shape[0]
+        terms = [(kept,), (received,)]
+
+        def total(start, span):
+            value = None
+            for term in terms:
+                parts = [
+                    lax.slice_in_dim(part, start, start + span, axis=0).astype(jnp.float32)
+                    for part in term
+                ]
+                if value is None:
+                    value = parts[0]
+                elif len(parts) == 1:
+                    value = low_precision(value + parts[0])
+                else:
+                    value = low_precision((value + parts[0]) + (parts[1] + parts[2]))
+            return value.astype(jnp.bfloat16)
+
+        for mask_even, mask_odd in ((2, 1), (1, 2)):
+            rows //= 2
+            terms.append((self.hop(total(rows, rows), mask_even, mask_odd),))
+        for bit, size in reversed(self.upper):
+            rows >>= size
+            terms.append(
+                tuple(
+                    self.hop(total(k * rows, rows), k << bit, k << bit) for k in range(1, 1 << size)
+                )
+            )
+        mine = total(0, rows)
+        step = 2
+        while step < self.ctx:
+            pairs = [(i, i ^ step) for i in range(self.ctx)]
+            other = lax.ppermute(mine, "ctx", pairs)
+            mine = low_precision(mine.astype(jnp.float32) + other.astype(jnp.float32)).astype(
+                jnp.bfloat16
+            )
+            step *= 2
+        return mine
+
+
+def order_table(links):
+    return jnp.concatenate(
+        [links.places(links.core), links.places(1 - links.core), links.core[None]]
+    ).astype(jnp.int32)
+
+
+def in_vmem(body, name, scalars, sources, out_shapes):
+    return pl.pallas_call(
+        body,
+        name=name,
+        out_shape=out_shapes,
+        in_specs=[pl.BlockSpec(memory_space=pltpu.SMEM)]
+        + [pl.BlockSpec(memory_space=pltpu.VMEM)] * len(sources),
+        out_specs=[pl.BlockSpec(memory_space=pltpu.VMEM)] * len(out_shapes),
+        compiler_params=pltpu.CompilerParams(vmem_limit_bytes=48 << 20),
+    )(scalars, *sources)
+
+
+def aligned(row, rows):
+    return pl.ds(pl.multiple_of(row, 8), rows)
+
+
+def assemble(links, name, mine, theirs, parts):
+    dp = links.dp
+    block = mine.shape[0] // dp
+
+    def body(scalar, mine_ref, theirs_ref, *outs):
+        def place(core):
+            for side, source in enumerate((mine_ref, theirs_ref)):
+                half = core if side == 0 else 1 - core
+
+                def one(position, carry):
+                    owner = scalar[side * dp + position]
+                    for out, (rows, columns, first) in zip(outs, parts):
+                        out[aligned(owner * rows, rows), pl.ds(half * columns, columns)] = source[
+                            aligned(position * block, rows), pl.ds(first, columns)
+                        ]
+                    return carry
+
+                lax.fori_loop(0, dp, one, 0)
+
+        for core in range(2):
+            pl.when(scalar[2 * dp] == core)(lambda core=core: place(core))
+
+    shapes = [
+        jax.ShapeDtypeStruct((dp * rows, 2 * columns), mine.dtype) for rows, columns, _ in parts
+    ]
+    return in_vmem(body, name, order_table(links), [mine, theirs], shapes)
+
+
+def split_up(links, name, wholes, parts):
+    dp = links.dp
+    block = max(rows for rows, _, _ in parts)
+    width = max(first + columns for _, columns, first in parts)
+
+    def body(scalar, *refs):
+        sources, outs = refs[: len(wholes)], refs[len(wholes) :]
+
+        def place(core):
+            for side, out in enumerate(outs):
+                half = core if side == 0 else 1 - core
+
+                def one(position, carry):
+                    owner = scalar[side * dp + position]
+                    for source, (rows, columns, first) in zip(sources, parts):
+                        out[aligned(position * block, rows), pl.ds(first, columns)] = source[
+                            aligned(owner * rows, rows), pl.ds(half * columns, columns)
+                        ].astype(jnp.bfloat16)
+                    return carry
+
+                lax.fori_loop(0, dp, one, 0)
+
+        for core in range(2):
+            pl.when(scalar[2 * dp] == core)(lambda core=core: place(core))
+
+    shapes = [jax.ShapeDtypeStruct((dp * block, width), jnp.bfloat16)] * 2
+    return in_vmem(body, name, order_table(links), wholes, shapes)
+
+
+def half_columns(links, value):
+    span = value.shape[1] // 2
+    return lax.dynamic_slice_in_dim(value, links.core * span, span, 1)
+
+
+def both_halves(links, mine, theirs):
+    even = links.core == 0
+    return jnp.concatenate(
+        [jnp.where(even, mine, theirs), jnp.where(even, theirs, mine)], axis=1
+    ).astype(jnp.float32)
+
+
+def whole_sequence(links, keys, values):
+    if links.ctx != 2:
+        return tuple(lax.all_gather(v, "ctx", axis=1, tiled=True) for v in (keys, values))
+    mine = jnp.concatenate([keys, values], axis=2)
+    theirs = links.swap(mine)
+    even = links.core == 0
+    both = jnp.concatenate(
+        [jnp.where(even, mine, theirs), jnp.where(even, theirs, mine)], axis=1
+    )
+    width = keys.shape[2]
+    return both[:, :, :width], both[:, :, width:]
+
+
+def own_block(links, grad_keys, grad_values):
+    grads = jnp.concatenate([grad_keys, grad_values], axis=1).astype(jnp.bfloat16)
+    if links.ctx != 2:
+        share = lax.psum_scatter(grads, "ctx", scatter_dimension=0, tiled=True)
+    else:
+        span = grads.shape[0] // 2
+        first, second = grads[:span], grads[span:]
+        even = links.core == 0
+        theirs = links.swap(jnp.where(even, second, first))
+        mine = jnp.where(even, first, second)
+        share = (mine.astype(jnp.float32) + theirs.astype(jnp.float32)).astype(jnp.bfloat16)
+    width = grad_keys.shape[1]
+    return share[:, :width], share[:, width:]
+
+
+def scatter(links, name, wholes, parts):
+    kept, sent = split_up(links, name, wholes, parts)
+    mine = links.reduce(kept, links.swap(sent))
+    theirs = links.swap(mine)
+    return [
+        both_halves(
+            links, mine[:rows, first : first + columns], theirs[:rows, first : first + columns]
+        )
+        for rows, columns, first in parts
+    ]
 
 
 def shards(
@@ -164,23 +383,44 @@
     positions = lax.axis_index("ctx") * ctx_tok + lax.iota(jnp.int32, ctx_tok)
     valid_rows = (positions[None, :] < lengths[:, None]).reshape(total_rows, 1)
     rows_in = tokens.reshape(total_rows, model_width)
-    attn_set = (
-        lax.all_gather(qkv_weight, "dp", axis=0, tiled=True),
-        lax.all_gather(query_bias, "dp", axis=0, tiled=True),
-        lax.all_gather(value_bias, "dp", axis=0, tiled=True),
-        lax.all_gather(out_weight, "dp", axis=0, tiled=True),
-        lax.all_gather(out_bias, "dp", axis=0, tiled=True),
-        lax.all_gather(norm1_gain, "dp", axis=0, tiled=True),
-        lax.all_gather(norm1_shift, "dp", axis=0, tiled=True),
-    )
-    ffn_set = (
-        lax.all_gather(up_weight, "dp", axis=0, tiled=True),
-        lax.all_gather(up_bias, "dp", axis=0, tiled=True),
-        lax.all_gather(down_weight, "dp", axis=0, tiled=True),
-        lax.all_gather(down_bias, "dp", axis=0, tiled=True),
-        lax.all_gather(norm2_gain, "dp", axis=0, tiled=True),
-        lax.all_gather(norm2_shift, "dp", axis=0, tiled=True),
-    )
+    links = Links()
+    shard_rows = qkv_weight.shape[0]
+    ff_rows = down_weight.shape[0]
+    up_columns = ff_rows // shard_rows
+    vectors = jnp.stack(
+        [query_bias, value_bias, out_bias, norm1_gain, norm1_shift]
+        + [down_bias, norm2_gain, norm2_shift]
+        + [up_bias[i * shard_rows : (i + 1) * shard_rows] for i in range(up_columns)],
+        axis=1,
+    )
+    vectors = jnp.pad(vectors, ((0, 0), (0, 128 - vectors.shape[1])))
+    attn_piece = jnp.concatenate(
+        [half_columns(links, qkv_weight), half_columns(links, out_weight), vectors], axis=1
+    )
+    qkv_half, out_half, up_half, down_half = (
+        weight.shape[1] // 2 for weight in (qkv_weight, out_weight, up_weight, down_weight)
+    )
+    attn_parts = [(shard_rows, qkv_half, 0), (shard_rows, out_half, qkv_half)]
+    up_parts = [(shard_rows, up_half, 0)]
+    down_parts = [(ff_rows, down_half, 0)]
+    attn_mine = links.gather(attn_piece)
+    qkv_full, out_full = assemble(
+        links, "attn_weights", attn_mine, links.swap(attn_mine), attn_parts
+    )
+    up_mine = links.gather(half_columns(links, up_weight))
+    (up_full,) = assemble(links, "up_weight", up_mine, links.swap(up_mine), up_parts)
+    down_mine = links.gather(half_columns(links, down_weight))
+    (down_full,) = assemble(links, "down_weight", down_mine, links.swap(down_mine), down_parts)
+    order = jnp.argsort(links.places(links.core))
+    vector_blocks = attn_mine[:, qkv_half + out_half :].reshape(links.dp, shard_rows, 128)[order]
+    vector_rows = jnp.transpose(vector_blocks, (2, 0, 1)).reshape(128, links.dp * shard_rows)
+    up_bias_full = jnp.transpose(
+        vector_rows[8 : 8 + up_columns].reshape(up_columns, links.dp, shard_rows), (1, 0, 2)
+    ).reshape(-1)
+    attn_set = (qkv_full, vector_rows[0], vector_rows[1], out_full) + tuple(
+        vector_rows[i] for i in (2, 3, 4)
+    )
+    ffn_set = (up_full, up_bias_full, down_full) + tuple(vector_rows[i] for i in (5, 6, 7))
     projected = matmul(rows_in, attn_set[0])
     query_rows = (projected[:, :model_width] + attn_set[1].astype(jnp.float32)).astype(jnp.bfloat16)
     key_rows = projected[:, model_width : 2 * model_width].astype(jnp.bfloat16)
@@ -189,10 +429,7 @@
     )
     key_local = key_rows.reshape(seq_dev, ctx_tok, model_width)
     value_local = value_rows.reshape(seq_dev, ctx_tok, model_width)
-    key_seq, value_seq = (
-        lax.all_gather(key_local, "ctx", axis=1, tiled=True),
-        lax.all_gather(value_local, "ctx", axis=1, tiled=True),
-    )
+    key_seq, value_seq = whole_sequence(links, key_local, value_local)
     query_seq = query_rows.reshape(seq_dev, ctx_tok, HEADS, head_dim)
     member = 0
     mixed_heads, log_total = attend_forward(
@@ -219,53 +456,13 @@
     output = layer_norm(
         resid2, ffn_set[4].astype(jnp.float32), ffn_set[5].astype(jnp.float32)
     ).astype(jnp.bfloat16)
-    totals = lax.psum(
-        (
-            jnp.sum(jnp.where(valid_rows, input_float * input_float, 0.0)),
-            jnp.sum(jnp.where(valid_rows, attn_branch * attn_branch, 0.0)),
-            jnp.sum(jnp.where(valid_rows, ffn_branch * ffn_branch, 0.0)),
-            jnp.sum(valid_rows.astype(jnp.float32)),
-        ),
-        ("ctx", "dp"),
-    )
-    stream_rms = jnp.sqrt(
-        jnp.stack([totals[0], totals[1], totals[2]]) / (totals[3] * model_width) + 1e-06
-    )
-    renewed = lax.optimization_barrier(
-        (
-            qkv_weight,
-            query_bias,
-            value_bias,
-            out_weight,
-            out_bias,
-            norm1_gain,
-            norm1_shift,
-            up_weight,
-            up_bias,
-            down_weight,
-            down_bias,
-            norm2_gain,
-            norm2_shift,
-            cotangent,
-        )
-    )
-    back_attn = (
-        lax.all_gather(renewed[0], "dp", axis=0, tiled=True),
-        lax.all_gather(renewed[1], "dp", axis=0, tiled=True),
-        lax.all_gather(renewed[2], "dp", axis=0, tiled=True),
-        lax.all_gather(renewed[3], "dp", axis=0, tiled=True),
-        lax.all_gather(renewed[4], "dp", axis=0, tiled=True),
-        lax.all_gather(renewed[5], "dp", axis=0, tiled=True),
-        lax.all_gather(renewed[6], "dp", axis=0, tiled=True),
-    )
-    back_ffn = (
-        lax.all_gather(renewed[7], "dp", axis=0, tiled=True),
-        lax.all_gather(renewed[8], "dp", axis=0, tiled=True),
-        lax.all_gather(renewed[9], "dp", axis=0, tiled=True),
-        lax.all_gather(renewed[10], "dp", axis=0, tiled=True),
-        lax.all_gather(renewed[11], "dp", axis=0, tiled=True),
-        lax.all_gather(renewed[12], "dp", axis=0, tiled=True),
-    )
+    totals = (
+        jnp.sum(jnp.where(valid_rows, input_float * input_float, 0.0)),
+        jnp.sum(jnp.where(valid_rows, attn_branch * attn_branch, 0.0)),
+        jnp.sum(jnp.where(valid_rows, ffn_branch * ffn_branch, 0.0)),
+        jnp.sum(valid_rows.astype(jnp.float32)),
+    )
+    back_attn, back_ffn = attn_set, ffn_set
     grad_rows = cotangent.reshape(total_rows, model_width).astype(jnp.float32)
     _, norm2_back = jax.vjp(
         layer_norm, resid2, back_ffn[4].astype(jnp.float32), back_ffn[5].astype(jnp.float32)
@@ -279,26 +476,8 @@
     grad_up = inner_rows(hidden_low, grad_upper)
     grad_up_bias = jnp.sum(grad_upper, axis=0, dtype=jnp.float32)
     grad_hidden1 = grad_resid2 + outer_rows(grad_upper, back_ffn[0])
-    ffn_grads = (
-        lax.psum_scatter(
-            grad_up.astype(jnp.bfloat16), "dp", scatter_dimension=0, tiled=True
-        ).astype(jnp.float32),
-        lax.psum_scatter(
-            grad_up_bias.astype(jnp.bfloat16), "dp", scatter_dimension=0, tiled=True
-        ).astype(jnp.float32),
-        lax.psum_scatter(
-            grad_down.astype(jnp.bfloat16), "dp", scatter_dimension=0, tiled=True
-        ).astype(jnp.float32),
-        lax.psum_scatter(
-            grad_down_bias.astype(jnp.bfloat16), "dp", scatter_dimension=0, tiled=True
-        ).astype(jnp.float32),
-        lax.psum_scatter(
-            grad_gain2.astype(jnp.bfloat16), "dp", scatter_dimension=0, tiled=True
-        ).astype(jnp.float32),
-        lax.psum_scatter(
-            grad_shift2.astype(jnp.bfloat16), "dp", scatter_dimension=0, tiled=True
-        ).astype(jnp.float32),
-    )
+    up_grad = scatter(links, "up_grad", [grad_up.astype(jnp.bfloat16)], up_parts)
+    down_grad = scatter(links, "down_grad", [grad_down.astype(jnp.bfloat16)], down_parts)
     _, norm1_back = jax.vjp(
         layer_norm, resid1, back_attn[5].astype(jnp.float32), back_attn[6].astype(jnp.float32)
     )
@@ -324,73 +503,51 @@
         key_span,
         score_scale,
     )
-    key_share = lax.psum_scatter(
-        grad_keys.astype(jnp.bfloat16), "ctx", scatter_dimension=0, tiled=True
-    )
-    value_share = lax.psum_scatter(
-        grad_values.astype(jnp.bfloat16), "ctx", scatter_dimension=0, tiled=True
-    )
+    key_share, value_share = own_block(links, grad_keys, grad_values)
     query_grads = grad_query.astype(jnp.bfloat16)
     grad_qkv_rows = jnp.concatenate([query_grads, key_share, value_share], axis=1)
     grad_qkv = inner_rows(rows_in, grad_qkv_rows)
     grad_query_bias = jnp.sum(grad_qkv_rows[:, :model_width], axis=0, dtype=jnp.float32)
     grad_value_bias = jnp.sum(grad_qkv_rows[:, 2 * model_width :], axis=0, dtype=jnp.float32)
     input_grad = grad_resid1 + outer_rows(grad_qkv_rows, back_attn[0])
-    attn_grads = (
-        lax.psum_scatter(
-            grad_qkv.astype(jnp.bfloat16), "dp", scatter_dimension=0, tiled=True
-        ).astype(jnp.float32),
-        lax.psum_scatter(
-            grad_query_bias.astype(jnp.bfloat16), "dp", scatter_dimension=0, tiled=True
-        ).astype(jnp.float32),
-        lax.psum_scatter(
-            grad_value_bias.astype(jnp.bfloat16), "dp", scatter_dimension=0, tiled=True
-        ).astype(jnp.float32),
-        lax.psum_scatter(
-            grad_out.astype(jnp.bfloat16), "dp", scatter_dimension=0, tiled=True
-        ).astype(jnp.float32),
-        lax.psum_scatter(
-            grad_out_bias.astype(jnp.bfloat16), "dp", scatter_dimension=0, tiled=True
-        ).astype(jnp.float32),
-        lax.psum_scatter(
-            grad_gain1.astype(jnp.bfloat16), "dp", scatter_dimension=0, tiled=True
-        ).astype(jnp.float32),
-        lax.psum_scatter(
-            grad_shift1.astype(jnp.bfloat16), "dp", scatter_dimension=0, tiled=True
-        ).astype(jnp.float32),
-    )
-    summed = (
-        lax.psum(attn_grads[0].astype(jnp.bfloat16), "ctx").astype(jnp.float32),
-        lax.psum(attn_grads[1].astype(jnp.bfloat16), "ctx").astype(jnp.float32),
-        lax.psum(attn_grads[2].astype(jnp.bfloat16), "ctx").astype(jnp.float32),
-        lax.psum(attn_grads[3].astype(jnp.bfloat16), "ctx").astype(jnp.float32),
-        lax.psum(attn_grads[4].astype(jnp.bfloat16), "ctx").astype(jnp.float32),
-        lax.psum(attn_grads[5].astype(jnp.bfloat16), "ctx").astype(jnp.float32),
-        lax.psum(attn_grads[6].astype(jnp.bfloat16), "ctx").astype(jnp.float32),
-        lax.psum(ffn_grads[0].astype(jnp.bfloat16), "ctx").astype(jnp.float32),
-        lax.psum(ffn_grads[1].astype(jnp.bfloat16), "ctx").astype(jnp.float32),
-        lax.psum(ffn_grads[2].astype(jnp.bfloat16), "ctx").astype(jnp.float32),
-        lax.psum(ffn_grads[3].astype(jnp.bfloat16), "ctx").astype(jnp.float32),
-        lax.psum(ffn_grads[4].astype(jnp.bfloat16), "ctx").astype(jnp.float32),
-        lax.psum(ffn_grads[5].astype(jnp.bfloat16), "ctx").astype(jnp.float32),
-    )
+    vector_grads = jnp.stack(
+        [grad_query_bias, grad_value_bias, grad_out_bias, grad_gain1, grad_shift1]
+        + [grad_down_bias, grad_gain2, grad_shift2]
+    )
+    up_bias_rows = jnp.transpose(
+        grad_up_bias.reshape(links.dp, up_columns, shard_rows), (1, 0, 2)
+    ).reshape(up_columns, model_width)
+    total_rows_4 = jnp.broadcast_to(jnp.stack(totals)[:, None], (4, model_width))
+    vector_grads = jnp.concatenate([vector_grads, up_bias_rows, total_rows_4])
+    vector_grads = jnp.pad(vector_grads, ((0, 128 - vector_grads.shape[0]), (0, 0)))
+    vector_grads = jnp.transpose(vector_grads).astype(jnp.bfloat16)
+    vector_grads = jnp.concatenate([vector_grads, vector_grads], axis=1)
+    attn_grad = scatter(
+        links,
+        "attn_grad",
+        [grad_qkv.astype(jnp.bfloat16), grad_out.astype(jnp.bfloat16), vector_grads],
+        attn_parts + [(shard_rows, 128, qkv_half + out_half)],
+    )
+    vector_sums = jnp.transpose(attn_grad[2][:, :128])
+    stream_sums = vector_sums[8 + up_columns : 12 + up_columns, 0]
+    stream_rms = jnp.sqrt(stream_sums[:3] / (stream_sums[3] * model_width) + 1e-06)
     return (
         output.reshape(seq_dev, ctx_tok, model_width),
         input_grad.reshape(seq_dev, ctx_tok, model_width),
         stream_rms,
-        summed[0],
-        summed[1],
-        summed[2],
-        summed[3],
-        summed[4],
-        summed[5],
-        summed[6],
-        summed[7],
-        summed[8],
-        summed[9],
-        summed[10],
-        summed[11],
-        summed[12],
+        attn_grad[0],
+        vector_sums[0],
+        vector_sums[1],
+        attn_grad[1],
+        vector_sums[2],
+        vector_sums[3],
+        vector_sums[4],
+        up_grad[0],
+        vector_sums[8 : 8 + up_columns].reshape(-1),
+        down_grad[0],
+        vector_sums[5],
+        vector_sums[6],
+        vector_sums[7],
     )
 
 

time: 1380 us -> 448 us (0.32)
  waiting for transfers between devices: 920 us -> 92.4 us
  blocking collectives: 195 us -> 0 us
  starting transfers between devices: 0.88 us -> 71.7 us
  Pallas kernels: 0 us -> 28.1 us
  matrix products: 149 us -> 128 us
  between operations: 18.9 us -> 3.16 us
    all_gather x10 -> x0, waiting for transfers between devices: 487 us -> none  [the longest x1 76.8 us: shards(): lax.all_gather(up_weight, 'dp', axis=0, tiled=True)]
    reduce_scatter x5 -> x0, waiting for transfers between devices: 412 us -> none  [the longest x1 142 us: shards(): lax.psum_scatter(grad_up.astype(jnp.bfloat16), 'dp', scatter_dimension=0,...]
    unnamed x2 -> x0, blocking collectives: 151 us -> none
    ppermute x0 -> x41, waiting for transfers between devices: none -> 92.4 us  [the longest x30 91.9 us: hop(): return lax.ppermute(value, ('ctx', 'dp'), pairs)]
    ppermute x0 -> x41, starting transfers between devices: none -> 71.7 us  [the longest x30 69.5 us: hop(): return lax.ppermute(value, ('ctx', 'dp'), pairs)]
    psum x2 -> x0, blocking collectives: 44.2 us -> none  [the longest x1 41.5 us: shards(): lax.psum((jnp.sum(jnp.where(valid_rows, input_float * input_float, 0.0)),...]
    pallas_call x0 -> x6, Pallas kernels: none -> 28.1 us  [in_vmem(): pl.pallas_call(body, name=name, out_shape=out_shapes, in_specs=[pl.BlockS...]
    psum x1 -> x0, waiting for transfers between devices: 15.7 us -> none  [shards(): lax.psum(attn_grads[0].astype(jnp.bfloat16), 'ctx').astype(jnp.float32)]
  transfers between devices with their start and end apart: 17 -> 41, of which waited for: 14 -> 15; matrix products, arithmetic and copies ran while one was open for 11% -> 19% of each run, Pallas kernels for 0% -> 6%
where the time goes in v1:
time: 448 us; the launch traced here: 440 us
  matrix products  128 us (29%)
  waiting for transfers between devices  92.4 us (21%)
  starting transfers between devices  71.7 us (16%)
  local copies, waits for them, and re-layouts  61.7 us (14%)
  other arithmetic  53.7 us (12%)
  Pallas kernels  28.1 us (6%)
    ppermute x30, waiting for transfers between devices, hop(): return lax.ppermute(value, ('ctx', 'dp'), pairs)  91.9 us
    ppermute x30, starting transfers between devices, hop(): return lax.ppermute(value, ('ctx', 'dp'), pairs)  69.5 us
    dot_general x4, matrix products, matmul(): return jnp.dot(left, right, preferred_element_type=jnp.float32)  29.3 us
    pallas_call x6, Pallas kernels, in_vmem(): pl.pallas_call(body, name=name, out_shape=out_shapes, in_specs=[pl.BlockS...  28.1 us
    dot_general x4, matrix products, outer_rows(): lax.dot_general(left, right, (((1,), (1,)), ((), ())), preferred_element_...  18.5 us
    dot_general x4, matrix products, inner_rows(): lax.dot_general(left, right, (((0,), (0,)), ((), ())), preferred_element_...  17 us
    dot_general x2, matrix products, second_sweep(): jnp.einsum('hqk,khd->qhd', weights, value_block, preferred_element_type=j...  14.1 us
    unnamed x101, local copies, waits for them, and re-layouts  13.8 us
  transfers between devices with their start and end apart: 41, of which 15 were waited for; matrix products, arithmetic and copies ran while one was open for 19% of the time, Pallas kernels for 6%

profile of v1, /device:TPU:0, one launch (start us, length us, event | category | flops | bytes accessed | tf_op | source)
XLA Modules:
  0.0 439.9 jit_solution(148412339719721746)
XLA Ops:
  25.5 6.9 %collective-permute-done.3 = bf16[192,1664]{1,0:T(8,128)(2,1)S(1)} collective-permute-done((bf16[192,1664]{1,0:T(8,128)(2,1)S(1)}, bf16[192,1664]{1,0:T(8,128)(2,1)S(1)}, u32[]{:S(2)}, u32[]{:S(2)}) %collective-permute-start.3) | collective-permute-done | bytes 639008 | tf_op jit(solution)/shard_map/ppermute | solution.py:168
  35.5 16.6 %collective-permute-start.13 = (bf16[192,384]{1,0:T(8,128)(2,1)S(1)}, bf16[192,384]{1,0:T(8,128)(2,1)S(1)}, u32[]{:S(2)}, u32[]{:S(2)}) collective-permute-start(bf16[192,384]{1,0:T(8,128)(2,1)S(1)} %get-tuple-element.310), channel_id=1, source_target_pairs={{0,4},{1,5},{2,6},{3,7},{4,0},{5,1},{6,2},{7,3},{8,12},{9,13},{10,... | collective-permute-start | bytes 442376 | tf_op jit(solution)/shard_map/ppermute | solution.py:168
  75.8 8.8 %collective-permute-done.11 = bf16[384,1536]{1,0:T(8,128)(2,1)} collective-permute-done((bf16[384,1536]{1,0:T(8,128)(2,1)}, bf16[384,1536]{1,0:T(8,128)(2,1)}, u32[]{:S(2)}, u32[]{:S(2)}) %collective-permute-start.11) | collective-permute-done | bytes 1179680 | tf_op jit(solution)/shard_map/ppermute | solution.py:168
  87.3 9.9 %collective-permute-done.17 = bf16[1536,384]{1,0:T(8,128)(2,1)} collective-permute-done((bf16[1536,384]{1,0:T(8,128)(2,1)}, bf16[1536,384]{1,0:T(8,128)(2,1)}, u32[]{:S(2)}, u32[]{:S(2)}) %collective-permute-start.17) | collective-permute-done | bytes 1179680 | tf_op jit(solution)/shard_map/ppermute | solution.py:168
  118.4 5.0 %up_weight.1 = bf16[768,3072]{1,0:T(8,128)(2,1)} custom-call(s32[33]{0:T(128)S(1)} %pad_add_fusion.scalar, bf16[768,1536]{1,0:T(8,128)(2,1)} %constant_dynamic-update-slice_fusion.18.mine_ref, bf16[768,1536]{1,0:T(8,128)(2,1)} %collective-permute-done.12.theirs_ref), custom_call_target="tpu_custom_call" | custom-call | tf_op jit(solution)/shard_map/up_weight/pallas_call | solution.py:235
  123.4 5.2 %down_weight.1 = bf16[3072,768]{1,0:T(8,128)(2,1)} custom-call(s32[33]{0:T(128)S(1)} %pad_add_fusion.scalar, bf16[3072,384]{1,0:T(8,128)(2,1)} %constant_dynamic-update-slice_fusion.29.mine_ref, bf16[3072,384]{1,0:T(8,128)(2,1)} %collective-permute-done.18.theirs_ref), custom_call_target="tpu_custom_call" | custom-call | tf_op jit(solution)/shard_map/down_weight/pallas_call | solution.py:235
  132.6 15.5 %while.36 = (s32[]{:T(128)}, f32[12,512]{1,0:T(8,128)S(1)}, f32[12,512]{1,0:T(8,128)S(1)}, s32[]{:T(128)}, s32[]{:T(128)}, /*index=5*/bf16[1024,768]{0,1:T(8,128...) while((s32[]{:T(128)}, f32[12,512]{1,0:T(8,128)S(1)}, ...), condition=%wide.region_4.5_spmd, body=%wide.region_1.4_spmd.sunk | while | flops 424686592 | bytes 28632752 | solution.py:76
  149.5 18.4 %while.37 = (s32[]{:T(128)}, f32[512,12,64]{0,2,1:T(8,128)}, s32[]{:T(128)}, bf16[1024,768]{0,1:T(8,128)(2,1)}, s32[]{:T(128)}, /*index=5*/bf16[1024,768]{0,1:T(...) while((s32[]{:T(128)}, f32[512,12,64]{0,2,1:T(8,128)}, ...), condition=%wide.region_6.7_spmd, body=%wide.region_5.6_spmd.sunk | while | flops 818283520 | bytes 8676535 | solution.py:88
  151.6 7.0 %bitcast_add_fusion.4 = f32[512,12,64]{0,2,1:T(8,128)} fusion(f32[512,12,64]{0,2,1:T(8,128)} %get-tuple-element.611, bf16[512,12,64]{0,2,1:T(8,128)(2,1)S(1)} %bitcast.185, f32[12,512]{1,0:T(8,128)S(1)} %get-tuple-element.629, pred[512]{0:T(512)(128)(4,1)S(1)} %add_compare_fusion.9, bf16[512,12,64]{0,2,1:T(8,128)(2,1)S(1)} %bitcast.184, ...), kind=kOutput, calls=%fused_computation.13.clone.1 | convolution fusion | flops 818282496 | bytes 5530112 | tf_op jit(solution)/shard_map/while/body/hqk,khd->qhd/dot_general | solution.py:84
  160.8 7.0 %bitcast_add_fusion.4 = f32[512,12,64]{0,2,1:T(8,128)} fusion(f32[512,12,64]{0,2,1:T(8,128)} %get-tuple-element.611, bf16[512,12,64]{0,2,1:T(8,128)(2,1)S(1)} %bitcast.185, f32[12,512]{1,0:T(8,128)S(1)} %get-tuple-element.629, pred[512]{0:T(512)(128)(4,1)S(1)} %add_compare_fusion.9, bf16[512,12,64]{0,2,1:T(8,128)(2,1)S(1)} %bitcast.184, ...), kind=kOutput, calls=%fused_computation.13.clone.1 | convolution fusion | flops 818282496 | bytes 5530112 | tf_op jit(solution)/shard_map/while/body/hqk,khd->qhd/dot_general | solution.py:84
  171.1 20.1 %multiply_convert_fusion.1 = (bf16[512,3072]{1,0:T(8,128)(2,1)S(1)}, f32[512,3072]{1,0:T(8,128)}, f32[512,3072]{1,0:T(8,128)}) fusion(f32[3072]{0:T(1024)S(1)} %reshape.305, bf16[768,3072]{1,0:T(8,128)(2,1)} %up_weight.1, f32[512,768]{1,0:T(8,128)S(1)} %get-tuple-element.314, f32[768]{0:T(1024)S(1)} %reshape.304, f32[768]{0:T(1024)S(1)} %reshape.303, ...), kind=kOutput, calls=%fused_computation.36 | convolution fusion | flops 2521694208 | bytes 22042624 | tf_op jit(solution)/shard_map/dot_general | solution.py:28
  198.4 9.3 %fusion.52 = (bf16[3072]{0:T(1024)(128)(2,1)S(1)}, bf16[512,3072]{1,0:T(8,128)(2,1)}) fusion(f32[512,3072]{1,0:T(8,128)} %get-tuple-element.312, f32[512,3072]{1,0:T(8,128)} %get-tuple-element.381, f32[3072]{0:T(1024)S(1)} %reshape.305, bf16[512,768]{1,0:T(8,128)(2,1)S(1)} %get-tuple-element.298, bf16[3072,768]{1,0:T(8,128)(2,1)S(1)} %bitcast.189), kind=kOutput, calls=%fused_computation.248 | convolution fusion | flops 2441081856 | bytes 21252096 | tf_op jit(solution)/shard_map/dot_general | solution.py:38
  207.8 5.1 %multiply_reduce_fusion = (bf16[768]{0:T(1024)(128)(2,1)S(1)}, f32[512]{0:T(512)S(1)}, bf16[768]{0:T(1024)(128)(2,1)S(1)}, f32[512,768]{1,0:T(8,128)S(1)}) fusion(f32[512,768]{1,0:T(8,128)S(1)} %get-tuple-element.314, f32[512]{0:T(512)S(1)} %fusion.40, f32[512]{0:T(512)S(1)} %broadcast_multiply_fusion.1, f32[768]{0:T(1024)S(1)} %reshape.303, ...), kind=kOutput, calls=%fused_computation.90 | convolution fusion | flops 2419849216 | bytes 12597248 | tf_op jit(solution)/shard_map/dot_general | solution.py:38
  223.1 55.3 %while.38 = (s32[]{:T(128)}, f32[512,12,64]{0,2,1:T(8,128)}, bf16[1024,768]{0,1:T(8,128)(2,1)}, bf16[1024,768]{0,1:T(8,128)(2,1)}, s32[]{:T(128)}, /*index=5*/bf...) while((s32[]{:T(128)}, f32[512,12,64]{0,2,1:T(8,128)}, ...), condition=%wide.region_17.18_spmd, body=%wide.region_16.17_spmd.sunk | while | flops 2046297088 | bytes 123545456 | solution.py:138
  228.9 5.8 %multiply_convert_fusion.3 = bf16[12,512,512]{2,1,0:T(8,128)(2,1)S(1)} fusion(f32[12,512,512]{2,1,0:T(8,128)S(1)} %fusion.128, f32[12,512]{1,0:T(8,128)S(1)} %get-tuple-element.677, f32[12,512]{1,0:T(8,128)S(1)} %get-tuple-element.674, pred[512]{0:T(512)(128)(4,1)S(1)} %add_compare_fusion.10, bf16[512,12,64]{0,2,1:T(8,128)(2,1)} %bitcast.179, ...), kind=kOutput, calls=%fused_computation.19.clone.1 | convolution fusion | flops 421527552 | bytes 20496896 | tf_op jit(solution)/shard_map/while/body/qhd,khd->hqk/dot_general | solution.py:108
  243.8 4.9 %convolution_multiply_fusion.2 = bf16[12,512,64]{1,2,0:T(8,128)(2,1)S(1)} fusion(bf16[12,512,512]{2,1,0:T(8,128)(2,1)} %copy-done.8, bf16[512,12,64]{0,2,1:T(8,128)(2,1)S(1)} %get-tuple-element.673), kind=kOutput, calls=%fused_computation.25.clone.1 | convolution fusion | flops 403439616 | bytes 7864320 | tf_op jit(solution)/shard_map/while/body/hqk,qhd->khd/dot_general | solution.py:116
  256.4 5.8 %multiply_convert_fusion.3 = bf16[12,512,512]{2,1,0:T(8,128)(2,1)S(1)} fusion(f32[12,512,512]{2,1,0:T(8,128)S(1)} %fusion.128, f32[12,512]{1,0:T(8,128)S(1)} %get-tuple-element.677, f32[12,512]{1,0:T(8,128)S(1)} %get-tuple-element.674, pred[512]{0:T(512)(128)(4,1)S(1)} %add_compare_fusion.10, bf16[512,12,64]{0,2,1:T(8,128)(2,1)} %bitcast.179, ...), kind=kOutput, calls=%fused_computation.19.clone.1 | convolution fusion | flops 421527552 | bytes 20496896 | tf_op jit(solution)/shard_map/while/body/qhd,khd->hqk/dot_general | solution.py:108
  319.6 5.6 %fusion.20.refs_0_ = bf16[768,2304]{1,0:T(8,128)(2,1)} fusion(bf16[512,1536]{0,1:T(8,128)(2,1)} %copy-done.22, bf16[512,768]{0,1:T(8,128)(2,1)} %bitcast.193, bf16[1,512,768]{2,1,0:T(8,128)(2,1)} %param.22), kind=kOutput, calls=%fused_computation.54 | convolution fusion | flops 1818427392 | bytes 6684672 | tf_op jit(solution)/shard_map/dot_general | solution.py:32
  335.5 12.5 %collective-permute-done.28 = bf16[384,1536]{1,0:T(8,128)(2,1)S(1)} collective-permute-done((bf16[384,1536]{1,0:T(8,128)(2,1)S(1)}, bf16[384,1536]{1,0:T(8,128)(2,1)S(1)}, u32[]{:S(2)}, u32[]{:S(2)}) %collective-permute-start.28) | collective-permute-done | bytes 1179680 | tf_op jit(solution)/shard_map/ppermute | solution.py:168
  350.7 16.3 %collective-permute-done.35 = bf16[1536,384]{1,0:T(8,128)(2,1)S(1)} collective-permute-done((bf16[1536,384]{1,0:T(8,128)(2,1)S(1)}, bf16[1536,384]{1,0:T(8,128)(2,1)S(1)}, u32[]{:S(2)}, u32[]{:S(2)}) %collective-permute-start.35) | collective-permute-done | bytes 1179680 | tf_op jit(solution)/shard_map/ppermute | solution.py:168
  376.7 10.2 %collective-permute-start.31 = (bf16[48,1536]{1,0:T(8,128)(2,1)S(1)}, bf16[48,1536]{1,0:T(8,128)(2,1)S(1)}, u32[]{:S(2)}, u32[]{:S(2)}) collective-permute-start(bf16[48,1536]{1,0:T(8,128)(2,1)S(1)} %get-tuple-element.331), channel_id=1, source_target_pairs={{0,8},{1,9},{2,10},{3,11},{4,12},{5,13},{6,14},{7,15},{8,0},{9,1},... | collective-permute-start | bytes 442376 | tf_op jit(solution)/shard_map/ppermute | solution.py:168
  389.8 7.6 %collective-permute-start.38 = (bf16[192,384]{1,0:T(8,128)(2,1)S(1)}, bf16[192,384]{1,0:T(8,128)(2,1)S(1)}, u32[]{:S(2)}, u32[]{:S(2)}) collective-permute-start(bf16[192,384]{1,0:T(8,128)(2,1)S(1)} %get-tuple-element.328), channel_id=1, source_target_pairs={{0,8},{1,9},{2,10},{3,11},{4,12},{5,13},{6,14},{7,15},{8,0},{9,1},... | collective-permute-start | bytes 442376 | tf_op jit(solution)/shard_map/ppermute | solution.py:168
  397.4 5.6 %collective-permute-done.31 = bf16[48,1536]{1,0:T(8,128)(2,1)S(1)} collective-permute-done((bf16[48,1536]{1,0:T(8,128)(2,1)S(1)}, bf16[48,1536]{1,0:T(8,128)(2,1)S(1)}, u32[]{:S(2)}, u32[]{:S(2)}) %collective-permute-start.31) | collective-permute-done | bytes 147488 | tf_op jit(solution)/shard_map/ppermute | solution.py:168
  424.3 8.5 %collective-permute-done.24 = bf16[48,1664]{1,0:T(8,128)(2,1)S(1)} collective-permute-done((bf16[48,1664]{1,0:T(8,128)(2,1)S(1)}, bf16[48,1664]{1,0:T(8,128)(2,1)S(1)}, u32[]{:S(2)}, u32[]{:S(2)}) %collective-permute-start.24) | collective-permute-done | bytes 159776 | tf_op jit(solution)/shard_map/ppermute | solution.py:168
  (356 shorter events, 252.1 us)
Async XLA Ops:
  11.2 42.2 %collective-permute-start.7 = (bf16[48,1536]{1,0:T(8,128)(2,1)S(1)}, bf16[48,1536]{1,0:T(8,128)(2,1)S(1)}, u32[]{:S(2)}, u32[]{:S(2)}) collective-permute-start(bf16[48,1536]{1,0:T(8,128)(2,1)S(1)} %get-tuple-element.316), channel_id=1, source_target_pairs={{0,4},{1,5},{2,6},{3,7},{4,0},{5,1},{6,2},{7,3},{8,12},{9,13},{10,... | collective-permute-start | bytes 442376 | tf_op jit(solution)/shard_map/ppermute | solution.py:168
  12.1 41.3 %collective-permute-start.8 = (bf16[48,1536]{1,0:T(8,128)(2,1)S(1)}, bf16[48,1536]{1,0:T(8,128)(2,1)S(1)}, u32[]{:S(2)}, u32[]{:S(2)}) collective-permute-start(bf16[48,1536]{1,0:T(8,128)(2,1)S(1)} %get-tuple-element.316), channel_id=1, source_target_pairs={{0,8},{1,9},{2,10},{3,11},{4,12},{5,13},{6,14},{7,15},{8,0},{9,1},... | collective-permute-start | bytes 442376 | tf_op jit(solution)/shard_map/ppermute | solution.py:168
  15.6 40.2 %collective-permute-start.9 = (bf16[48,1536]{1,0:T(8,128)(2,1)S(1)}, bf16[48,1536]{1,0:T(8,128)(2,1)S(1)}, u32[]{:S(2)}, u32[]{:S(2)}) collective-permute-start(bf16[48,1536]{1,0:T(8,128)(2,1)S(1)} %get-tuple-element.316), channel_id=1, source_target_pairs={{0,12},{1,13},{2,14},{3,15},{4,8},{5,9},{6,10},{7,11},{8,4},{9,5},... | collective-permute-start | bytes 442376 | tf_op jit(solution)/shard_map/ppermute | solution.py:168
  33.3 31.9 %collective-permute-start.4 = (bf16[384,1664]{1,0:T(8,128)(2,1)}, bf16[384,1664]{1,0:T(8,128)(2,1)S(1)}, u32[]{:S(2)}, u32[]{:S(2)}) collective-permute-start(bf16[384,1664]{1,0:T(8,128)(2,1)} %get-tuple-element.341), channel_id=1, source_target_pairs={{0,2},{1,3},{2,0},{3,1},{4,6},{5,7},{6,4},{7,5},{8,10},{9,11},{10,... | collective-permute-start | bytes 3833864 | tf_op jit(solution)/shard_map/ppermute | solution.py:168
  35.5 21.9 %collective-permute-start.13 = (bf16[192,384]{1,0:T(8,128)(2,1)S(1)}, bf16[192,384]{1,0:T(8,128)(2,1)S(1)}, u32[]{:S(2)}, u32[]{:S(2)}) collective-permute-start(bf16[192,384]{1,0:T(8,128)(2,1)S(1)} %get-tuple-element.310), channel_id=1, source_target_pairs={{0,4},{1,5},{2,6},{3,7},{4,0},{5,1},{6,2},{7,3},{8,12},{9,13},{10,... | collective-permute-start | bytes 442376 | tf_op jit(solution)/shard_map/ppermute | solution.py:168
  65.3 37.4 %collective-permute-start.5 = (bf16[768,1664]{1,0:T(8,128)(2,1)S(1)}, bf16[768,1664]{1,0:T(8,128)(2,1)}, u32[]{:S(2)}, u32[]{:S(2)}) collective-permute-start(bf16[768,1664]{1,0:T(8,128)(2,1)S(1)} %constant_dynamic-update-slice_fusion.7.mine_ref), channel_id=1, source_target_pairs={{0,16},{16,0},{1,17},{17,1},{2,18},{18,2},{3,19},{19,3},{4,20},{20... | collective-permute-start | bytes 7667720 | tf_op jit(solution)/shard_map/ppermute | solution.py:161
  68.1 16.5 %collective-permute-start.11 = (bf16[384,1536]{1,0:T(8,128)(2,1)}, bf16[384,1536]{1,0:T(8,128)(2,1)}, u32[]{:S(2)}, u32[]{:S(2)}) collective-permute-start(bf16[384,1536]{1,0:T(8,128)(2,1)} %get-tuple-element.345), channel_id=1, source_target_pairs={{0,2},{1,3},{2,0},{3,1},{4,6},{5,7},{6,4},{7,5},{8,10},{9,11},{10,... | collective-permute-start | bytes 3538952 | tf_op jit(solution)/shard_map/ppermute | solution.py:168
  73.9 23.3 %collective-permute-start.17 = (bf16[1536,384]{1,0:T(8,128)(2,1)}, bf16[1536,384]{1,0:T(8,128)(2,1)}, u32[]{:S(2)}, u32[]{:S(2)}) collective-permute-start(bf16[1536,384]{1,0:T(8,128)(2,1)} %get-tuple-element.343), channel_id=1, source_target_pairs={{0,2},{1,3},{2,0},{3,1},{4,6},{5,7},{6,4},{7,5},{8,10},{9,11},{10,... | collective-permute-start | bytes 3538952 | tf_op jit(solution)/shard_map/ppermute | solution.py:168
  86.9 31.4 %collective-permute-start.12 = (bf16[768,1536]{1,0:T(8,128)(2,1)}, bf16[768,1536]{1,0:T(8,128)(2,1)}, u32[]{:S(2)}, u32[]{:S(2)}) collective-permute-start(bf16[768,1536]{1,0:T(8,128)(2,1)} %constant_dynamic-update-slice_fusion.18.mine_ref), channel_id=1, source_target_pairs={{0,16},{16,0},{1,17},{17,1},{2,18},{18,2},{3,19},{19,3},{4,20},{20... | collective-permute-start | bytes 7077896 | tf_op jit(solution)/shard_map/ppermute | solution.py:161
  99.6 23.7 %collective-permute-start.18 = (bf16[3072,384]{1,0:T(8,128)(2,1)}, bf16[3072,384]{1,0:T(8,128)(2,1)}, u32[]{:S(2)}, u32[]{:S(2)}) collective-permute-start(bf16[3072,384]{1,0:T(8,128)(2,1)} %constant_dynamic-update-slice_fusion.29.mine_ref), channel_id=1, source_target_pairs={{0,16},{16,0},{1,17},{17,1},{2,18},{18,2},{3,19},{19,3},{4,20},{20... | collective-permute-start | bytes 7077896 | tf_op jit(solution)/shard_map/ppermute | solution.py:161
  282.0 28.9 %collective-permute-start.19 = (bf16[512,1536]{0,1:T(8,128)(2,1)}, bf16[512,1536]{0,1:T(8,128)(2,1)}, u32[]{:S(2)}, u32[]{:S(2)}) collective-permute-start(bf16[512,1536]{0,1:T(8,128)(2,1)} %broadcast_select_fusion), channel_id=1, source_target_pairs={{0,16},{16,0},{1,17},{17,1},{2,18},{18,2},{3,19},{19,3},{4,20},{20... | collective-permute-start | bytes 4718600 | tf_op jit(solution)/shard_map/ppermute | solution.py:161
  291.5 38.6 %collective-permute-start.27 = (bf16[768,1536]{1,0:T(8,128)(2,1)}, bf16[768,1536]{1,0:T(8,128)(2,1)}, u32[]{:S(2)}, u32[]{:S(2)}) collective-permute-start(bf16[768,1536]{1,0:T(8,128)(2,1)} %get-tuple-element.184), channel_id=1, source_target_pairs={{0,16},{16,0},{1,17},{17,1},{2,18},{18,2},{3,19},{19,3},{4,20},{20... | collective-permute-start | bytes 7077896 | tf_op jit(solution)/shard_map/ppermute | solution.py:161
  300.8 31.5 %collective-permute-start.34 = (bf16[3072,384]{1,0:T(8,128)(2,1)}, bf16[3072,384]{1,0:T(8,128)(2,1)}, u32[]{:S(2)}, u32[]{:S(2)}) collective-permute-start(bf16[3072,384]{1,0:T(8,128)(2,1)} %get-tuple-element.186), channel_id=1, source_target_pairs={{0,16},{16,0},{1,17},{17,1},{2,18},{18,2},{3,19},{19,3},{4,20},{20... | collective-permute-start | bytes 7077896 | tf_op jit(solution)/shard_map/ppermute | solution.py:161
  329.8 39.8 %collective-permute-start.20 = (bf16[768,1664]{1,0:T(8,128)(2,1)}, bf16[768,1664]{1,0:T(8,128)(2,1)S(1)}, u32[]{:S(2)}, u32[]{:S(2)}) collective-permute-start(bf16[768,1664]{1,0:T(8,128)(2,1)} %get-tuple-element.182), channel_id=1, source_target_pairs={{0,16},{16,0},{1,17},{17,1},{2,18},{18,2},{3,19},{19,3},{4,20},{20... | collective-permute-start | bytes 7667720 | tf_op jit(solution)/shard_map/ppermute | solution.py:161
  331.7 16.3 %collective-permute-start.28 = (bf16[384,1536]{1,0:T(8,128)(2,1)S(1)}, bf16[384,1536]{1,0:T(8,128)(2,1)S(1)}, u32[]{:S(2)}, u32[]{:S(2)}) collective-permute-start(bf16[384,1536]{1,0:T(8,128)(2,1)S(1)} %reduce-precision_convert_fusion.2), channel_id=1, source_target_pairs={{0,2},{1,3},{2,0},{3,1},{4,6},{5,7},{6,4},{7,5},{8,10},{9,11},{10,... | collective-permute-start | bytes 3538952 | tf_op jit(solution)/shard_map/ppermute | solution.py:168
  333.9 33.1 %collective-permute-start.35 = (bf16[1536,384]{1,0:T(8,128)(2,1)S(1)}, bf16[1536,384]{1,0:T(8,128)(2,1)S(1)}, u32[]{:S(2)}, u32[]{:S(2)}) collective-permute-start(bf16[1536,384]{1,0:T(8,128)(2,1)S(1)} %reduce-precision_convert_fusion.1), channel_id=1, source_target_pairs={{0,2},{1,3},{2,0},{3,1},{4,6},{5,7},{6,4},{7,5},{8,10},{9,11},{10,... | collective-permute-start | bytes 3538952 | tf_op jit(solution)/shard_map/ppermute | solution.py:168
  349.5 24.0 %collective-permute-start.29 = (bf16[192,1536]{1,0:T(8,128)(2,1)S(1)}, bf16[192,1536]{1,0:T(8,128)(2,1)S(1)}, u32[]{:S(2)}, u32[]{:S(2)}) collective-permute-start(bf16[192,1536]{1,0:T(8,128)(2,1)S(1)} %reduce-precision_convert_fusion.5), channel_id=1, source_target_pairs={{0,1},{1,0},{2,3},{3,2},{4,5},{5,4},{6,7},{7,6},{8,9},{9,8},{10,11... | collective-permute-start | bytes 1769480 | tf_op jit(solution)/shard_map/ppermute | solution.py:168
  368.4 18.5 %collective-permute-start.36 = (bf16[768,384]{1,0:T(8,128)(2,1)S(1)}, bf16[768,384]{1,0:T(8,128)(2,1)S(1)}, u32[]{:S(2)}, u32[]{:S(2)}) collective-permute-start(bf16[768,384]{1,0:T(8,128)(2,1)S(1)} %reduce-precision_convert_fusion.4), channel_id=1, source_target_pairs={{0,1},{1,0},{2,3},{3,2},{4,5},{5,4},{6,7},{7,6},{8,9},{9,8},{10,11... | collective-permute-start | bytes 1769480 | tf_op jit(solution)/shard_map/ppermute | solution.py:168
  369.9 34.3 %collective-permute-start.21 = (bf16[384,1664]{1,0:T(8,128)(2,1)S(1)}, bf16[384,1664]{1,0:T(8,128)(2,1)S(1)}, u32[]{:S(2)}, u32[]{:S(2)}) collective-permute-start(bf16[384,1664]{1,0:T(8,128)(2,1)S(1)} %reduce-precision_convert_fusion), channel_id=1, source_target_pairs={{0,2},{1,3},{2,0},{3,1},{4,6},{5,7},{6,4},{7,5},{8,10},{9,11},{10,... | collective-permute-start | bytes 3833864 | tf_op jit(solution)/shard_map/ppermute | solution.py:168
  376.7 26.3 %collective-permute-start.31 = (bf16[48,1536]{1,0:T(8,128)(2,1)S(1)}, bf16[48,1536]{1,0:T(8,128)(2,1)S(1)}, u32[]{:S(2)}, u32[]{:S(2)}) collective-permute-start(bf16[48,1536]{1,0:T(8,128)(2,1)S(1)} %get-tuple-element.331), channel_id=1, source_target_pairs={{0,8},{1,9},{2,10},{3,11},{4,12},{5,13},{6,14},{7,15},{8,0},{9,1},... | collective-permute-start | bytes 442376 | tf_op jit(solution)/shard_map/ppermute | solution.py:168
  386.9 16.1 %collective-permute-start.30 = (bf16[48,1536]{1,0:T(8,128)(2,1)S(1)}, bf16[48,1536]{1,0:T(8,128)(2,1)S(1)}, u32[]{:S(2)}, u32[]{:S(2)}) collective-permute-start(bf16[48,1536]{1,0:T(8,128)(2,1)S(1)} %get-tuple-element.329), channel_id=1, source_target_pairs={{0,4},{1,5},{2,6},{3,7},{4,0},{5,1},{6,2},{7,3},{8,12},{9,13},{10,... | collective-permute-start | bytes 442376 | tf_op jit(solution)/shard_map/ppermute | solution.py:168
  388.2 17.2 %collective-permute-start.39 = (bf16[192,384]{1,0:T(8,128)(2,1)S(1)}, bf16[192,384]{1,0:T(8,128)(2,1)S(1)}, u32[]{:S(2)}, u32[]{:S(2)}) collective-permute-start(bf16[192,384]{1,0:T(8,128)(2,1)S(1)} %get-tuple-element.327), channel_id=1, source_target_pairs={{0,12},{1,13},{2,14},{3,15},{4,8},{5,9},{6,10},{7,11},{8,4},{9,5},... | collective-permute-start | bytes 442376 | tf_op jit(solution)/shard_map/ppermute | solution.py:168
  389.8 18.5 %collective-permute-start.38 = (bf16[192,384]{1,0:T(8,128)(2,1)S(1)}, bf16[192,384]{1,0:T(8,128)(2,1)S(1)}, u32[]{:S(2)}, u32[]{:S(2)}) collective-permute-start(bf16[192,384]{1,0:T(8,128)(2,1)S(1)} %get-tuple-element.328), channel_id=1, source_target_pairs={{0,8},{1,9},{2,10},{3,11},{4,12},{5,13},{6,14},{7,15},{8,0},{9,1},... | collective-permute-start | bytes 442376 | tf_op jit(solution)/shard_map/ppermute | solution.py:168
  410.8 22.2 %collective-permute-start.40 = (bf16[192,384]{1,0:T(8,128)(2,1)S(1)}, bf16[192,384]{1,0:T(8,128)(2,1)S(1)}, u32[]{:S(2)}, u32[]{:S(2)}) collective-permute-start(bf16[192,384]{1,0:T(8,128)(2,1)S(1)} %reduce-precision_convert_fusion.10), channel_id=1, source_target_pairs={{0,16},{16,0},{1,17},{17,1},{2,18},{18,2},{3,19},{19,3},{4,20},{20... | collective-permute-start | bytes 442376 | tf_op jit(solution)/shard_map/ppermute | solution.py:161
  (71 other events, 733.5 us)

commit v2 on v1

v2 whole, which is shorter than its diff:
```python
import math

import jax
import jax.numpy as jnp
from jax import lax
from jax.experimental import pallas as pl
from jax.experimental.pallas import tpu as pltpu
from jax.sharding import PartitionSpec as P

HEADS = 12
LANES = 128
VECTORS = 16

masked_score = -1e30
norm_eps = 1e-05
f32 = jnp.float32
bf16 = jnp.bfloat16


def low_precision(value):
    return lax.reduce_precision(value, exponent_bits=8, mantissa_bits=7)


class Links:
    def __init__(self):
        self.dp = lax.axis_size("dp")
        self.ctx = lax.axis_size("ctx")
        self.bits = self.dp.bit_length() - 1
        assert self.dp == 1 << self.bits and self.bits >= 2 and self.ctx % 2 == 0
        self.core = lax.axis_index("ctx") % 2
        self.me = lax.axis_index("dp")
        self.upper = []
        bit = 2
        while bit < self.bits:
            self.upper.append((bit, min(2, self.bits - bit)))
            bit += 2

    def swap(self, value):
        return lax.ppermute(value, "ctx", [(i, i ^ 1) for i in range(self.ctx)])

    def hop(self, value, mask_even, mask_odd):
        pairs = []
        for block in range(self.ctx):
            mask = mask_odd if block % 2 else mask_even
            pairs += [(block * self.dp + i, block * self.dp + (i ^ mask)) for i in range(self.dp)]
        return lax.ppermute(value, ("ctx", "dp"), pairs)

    def places(self, core):
        position = lax.iota(jnp.int32, self.dp)
        quarter = self.dp // 4
        first = (position // quarter) % 2
        second = position // (2 * quarter)
        mask = (position % quarter) * 4 + first * (1 + core) + second * (2 - core)
        return jnp.bitwise_xor(self.me, mask)

    def spots(self, core):
        mask = jnp.bitwise_xor(self.me, lax.iota(jnp.int32, self.dp))
        low, high = mask % 2, (mask // 2) % 2
        first = jnp.where(core == 0, low, high)
        second = jnp.where(core == 0, high, low)
        quarter = self.dp // 4
        return mask // 4 + first * quarter + second * (2 * quarter)

    def table(self, *more):
        parts = [self.places(self.core), self.places(1 - self.core)]
        parts += [self.spots(self.core), self.spots(1 - self.core)]
        parts += [jnp.reshape(value, (1,)) for value in (self.core,) + more]
        return jnp.concatenate(parts).astype(jnp.int32)

    def gather(self, piece):
        held = piece
        for bit, size in self.upper:
            held = jnp.concatenate(
                [held] + [self.hop(held, k << bit, k << bit) for k in range(1, 1 << size)], axis=0
            )
        held = jnp.concatenate([held, self.hop(held, 1, 2)], axis=0)
        return jnp.concatenate([held, self.hop(held, 2, 1)], axis=0)

    def reduce(self, kept, received):
        rows = kept.shape[0]
        terms = [(kept,), (received,)]

        def total(start, span):
            value = None
            for term in terms:
                parts = [
                    lax.slice_in_dim(part, start, start + span, axis=0).astype(f32)
                    for part in term
                ]
                if value is None:
                    value = parts[0]
                elif len(parts) == 1:
                    value = low_precision(value + parts[0])
                else:
                    value = low_precision((value + parts[0]) + (parts[1] + parts[2]))
            return value.astype(bf16)

        for mask_even, mask_odd in ((2, 1), (1, 2)):
            rows //= 2
            terms.append((self.hop(total(rows, rows), mask_even, mask_odd),))
        for bit, size in reversed(self.upper):
            rows >>= size
            terms.append(
                tuple(
                    self.hop(total(k * rows, rows), k << bit, k << bit) for k in range(1, 1 << size)
                )
            )
        mine = total(0, rows)
        step = 2
        while step < self.ctx:
            pairs = [(i, i ^ step) for i in range(self.ctx)]
            other = lax.ppermute(mine, "ctx", pairs)
            mine = low_precision(mine.astype(f32) + other.astype(f32)).astype(bf16)
            step *= 2
        return mine


def half_columns(links, value):
    span = value.shape[1] // 2
    return lax.dynamic_slice_in_dim(value, links.core * span, span, 1)


def both_halves(links, mine, theirs):
    even = links.core == 0
    return jnp.concatenate(
        [jnp.where(even, mine, theirs), jnp.where(even, theirs, mine)], axis=1
    ).astype(f32)


def dot(left, right):
    return jnp.dot(left, right, preferred_element_type=f32)


def dot_rows(left, right):
    return lax.dot_general(left, right, (((1,), (1,)), ((), ())), preferred_element_type=f32)


def turned(value):
    return jnp.transpose(value)


def aligned(start, size, unit):
    return pl.ds(pl.multiple_of(start, unit), size)


SMEM = pl.BlockSpec(memory_space=pltpu.SMEM)
ANY = pl.BlockSpec(memory_space=pl.ANY)
VMEM = pl.BlockSpec(memory_space=pltpu.VMEM)


def call(body, name, sources, in_specs, outs, scratch=(), cost=None):
    return pl.pallas_call(
        body,
        name=name,
        out_shape=outs,
        in_specs=in_specs,
        out_specs=[VMEM] * len(outs),
        scratch_shapes=list(scratch),
        compiler_params=pltpu.CompilerParams(vmem_limit_bytes=56 << 20),
        cost_estimate=cost,
    )(*sources)


def shape(rows, columns, dtype):
    return jax.ShapeDtypeStruct((rows, columns), dtype)


class Piece:
    def __init__(self, dp, rows, columns, first):
        self.dp, self.rows, self.columns, self.first = dp, rows, columns, first

    def fetch(self, scalar, sides, whole, sem):
        core = scalar[4 * self.dp]
        for side, source in enumerate(sides):
            half = core if side == 0 else 1 - core

            def one(position, carry, side=side, source=source, half=half):
                owner = scalar[side * self.dp + position]
                pltpu.make_async_copy(
                    source.at[
                        aligned(position * self.rows, self.rows, 8),
                        pl.ds(self.first, self.columns),
                    ],
                    whole.at[
                        aligned(owner * self.rows, self.rows, 8),
                        aligned(half * self.columns, self.columns, LANES),
                    ],
                    sem,
                ).start()
                return carry

            lax.fori_loop(0, self.dp, one, 0)

    def ready(self, whole, sem):
        pltpu.make_async_copy(whole, whole, sem).wait()

    def whole(self):
        return pltpu.VMEM((self.dp * self.rows, 2 * self.columns), bf16)


def spread(scalar, dp, side, tile, out, rows, columns, tile_columns, base):
    count = tile.shape[0] // rows

    def one(i, carry):
        spot = scalar[(2 + side) * dp + base + i]
        out[aligned(spot * rows, rows, 8), columns] = tile[
            aligned(i * rows, rows, 8), tile_columns
        ].astype(bf16)
        return carry

    lax.fori_loop(0, count, one, 0)


def project(links, table, rows, mine, theirs, qkv_piece, vector_piece, scale):
    tokens, width = rows.shape

    def body(scalar, rows_ref, mine_ref, theirs_ref, q_ref, kv_ref, vec_ref, weight, vecs, sems):
        qkv_piece.fetch(scalar, (mine_ref, theirs_ref), weight, sems.at[0])
        core = scalar[4 * links.dp]

        def one(position, carry):
            owner = scalar[position]
            pltpu.make_async_copy(
                mine_ref.at[
                    aligned(position * vector_piece.rows, vector_piece.rows, 8),
                    pl.ds(vector_piece.first, LANES),
                ],
                vecs.at[aligned(owner * vector_piece.rows, vector_piece.rows, 8), :],
                sems.at[1],
            ).start()
            return carry

        lax.fori_loop(0, links.dp, one, 0)
        pltpu.make_async_copy(vecs, vecs, sems.at[1]).wait()
        vectors = turned(vecs[...].astype(f32))[:VECTORS]
        vec_ref[...] = vectors
        qkv_piece.ready(weight, sems.at[0])
        x = rows_ref[...]
        query = (dot(x, weight[:, :width]) + vectors[0:1]).astype(bf16)
        q_ref[...] = (query.astype(f32) * scale).astype(bf16)
        kv_ref[:, :width] = dot(x, weight[:, width : 2 * width]).astype(bf16)
        kv_ref[:, width:] = (dot(x, weight[:, 2 * width :]) + vectors[1:2]).astype(bf16)

    return call(
        body,
        "qkv",
        [table, rows, mine, theirs],
        [SMEM, VMEM, ANY, ANY],
        [shape(tokens, width, bf16), shape(tokens, 2 * width, bf16), shape(VECTORS, width, f32)],
        [qkv_piece.whole(), pltpu.VMEM((width, LANES), bf16), pltpu.SemaphoreType.DMA((2,))],
    )


def pair_specs(parts, pairs):
    specs = []
    for part in parts:
        rows = part.shape[0]
        specs.append(pl.BlockSpec((rows, LANES), lambda p, s: (0, p)))
        specs.append(pl.BlockSpec((rows, LANES), lambda p, s, pairs=pairs: (0, pairs + p)))
    return specs


def first_lanes(shape_, count):
    return (lax.broadcasted_iota(jnp.int32, shape_, 1) < count).astype(f32).astype(bf16)


def head_blocks(query):
    lane = lax.broadcasted_iota(jnp.int32, query.shape, 1)
    zero = jnp.zeros_like(query)
    half = LANES // 2
    return jnp.concatenate(
        [jnp.where(lane < half, query, zero), jnp.where(lane >= half, query, zero)], axis=0
    )


def attend(query, parts, starts, length):
    tokens, width = query.shape
    pairs = width // LANES
    span = sum(part.shape[0] for part in parts)
    half = LANES // 2
    chunk = min(256, tokens)
    scalars = jnp.concatenate(
        [jnp.reshape(v, (1,)).astype(jnp.int32) for v in [length, *starts]]
    )

    def body(scalar, q_ref, *refs):
        kv_refs = refs[: 2 * len(parts)]
        mixed_t_ref, mixed_ref, p_ref, inverse_ref, bias = refs[2 * len(parts) :]

        @pl.when(pl.program_id(0) == 0)
        def _():
            at = 0
            for i, part in enumerate(parts):
                rows = part.shape[0]
                position = scalar[1 + i] + lax.broadcasted_iota(jnp.int32, (rows, LANES), 0)
                lane = lax.broadcasted_iota(jnp.int32, (rows, LANES), 1)
                hidden = jnp.where(position < scalar[0], 0.0, masked_score)
                bias[at : at + rows, :] = jnp.where(lane == 0, hidden, 0.0).astype(bf16)
                at += rows

        keys = jnp.concatenate([ref[...] for ref in kv_refs[0::2]], axis=0)
        values = jnp.concatenate([ref[...] for ref in kv_refs[1::2]], axis=0)
        keys = jnp.concatenate([keys, bias[...]], axis=1)
        values_t = jnp.concatenate([turned(values), jnp.ones((16, span), bf16)], axis=0)
        queries = head_blocks(q_ref[...])
        queries = jnp.concatenate([queries, first_lanes(queries.shape, 1)], axis=1)
        for at in range(0, 2 * tokens, chunk):
            scores = dot_rows(keys, queries[at : at + chunk])
            peak = jnp.max(scores, axis=0, keepdims=True)
            weights = jnp.exp(scores - peak).astype(bf16)
            p_ref[:, at : at + chunk] = weights
            sums = dot(values_t, weights)
            inverse = 1.0 / sums[LANES : LANES + 1]
            inverse_ref[:, at : at + chunk] = inverse
            low = 0 if at < tokens else half
            to = at % tokens
            mixed_t_ref[low : low + half, to : to + chunk] = sums[low : low + half] * inverse
        mixed_ref[...] = turned(mixed_t_ref[...]).astype(bf16)

    sources = [query]
    for part in parts:
        sources += [part, part]
    return pl.pallas_call(
        body,
        name="attend",
        out_shape=[
            shape(width, tokens, f32),
            shape(tokens, width, bf16),
            jax.ShapeDtypeStruct((pairs, span, 2 * tokens), bf16),
            jax.ShapeDtypeStruct((pairs, 1, 2 * tokens), f32),
        ],
        grid_spec=pltpu.PrefetchScalarGridSpec(
            num_scalar_prefetch=1,
            grid=(pairs,),
            in_specs=[pl.BlockSpec((tokens, LANES), lambda p, s: (0, p))]
            + pair_specs(parts, pairs),
            out_specs=[
                pl.BlockSpec((LANES, tokens), lambda p, s: (p, 0)),
                pl.BlockSpec((tokens, LANES), lambda p, s: (0, p)),
                pl.BlockSpec((None, span, 2 * tokens), lambda p, s: (p, 0, 0)),
                pl.BlockSpec((None, 1, 2 * tokens), lambda p, s: (p, 0, 0)),
            ],
            scratch_shapes=[pltpu.VMEM((span, LANES), bf16)],
        ),
        compiler_params=pltpu.CompilerParams(vmem_limit_bytes=56 << 20),
    )(scalars, *sources)


def attend_back(query, parts, grad_mixed, mixed_t, weights, inverse, scale):
    tokens, width = query.shape
    pairs = width // LANES
    span = sum(part.shape[0] for part in parts)
    half = LANES // 2
    chunk = min(256, tokens)

    def body(_, q_ref, gm_ref, mt_ref, p_ref, inv_ref, *refs):
        kv_refs = refs[: 2 * len(parts)]
        dq_ref = refs[2 * len(parts)]
        dkv_refs = refs[2 * len(parts) + 1 : -1]
        ds_ref = refs[-1]
        keys = jnp.concatenate([ref[...] for ref in kv_refs[0::2]], axis=0)
        values = jnp.concatenate([ref[...] for ref in kv_refs[1::2]], axis=0)
        grads = turned(gm_ref[...].astype(f32))
        inv = inv_ref[...]
        product = grads * mt_ref[...]
        empty = jnp.zeros((half, tokens), bf16)
        even, odd = inv[:, :tokens], inv[:, tokens:]
        delta = jnp.concatenate(
            [
                jnp.sum(product[:half], axis=0, keepdims=True) * even,
                jnp.sum(product[half:], axis=0, keepdims=True) * odd,
            ],
            axis=1,
        )
        top = jnp.concatenate([(grads[:half] * even).astype(bf16), empty], axis=1)
        bottom = jnp.concatenate([empty, (grads[half:] * odd).astype(bf16)], axis=1)
        scaled = jnp.concatenate([top, bottom], axis=0)
        first = (-delta).astype(bf16).astype(f32)
        second = (-delta - first).astype(bf16).astype(f32)
        third = (-delta - first - second).astype(bf16).astype(f32)
        row = lax.broadcasted_iota(jnp.int32, (LANES, 2 * tokens), 0)
        limbs = jnp.where(
            row == 0, first, jnp.where(row == 1, second, jnp.where(row == 2, third, 0.0))
        ).astype(bf16)
        right = jnp.concatenate([scaled, limbs], axis=0)
        left = jnp.concatenate([values, first_lanes(values.shape, 3)], axis=1)
        for at in range(0, 2 * tokens, chunk):
            grad_probs = dot(left, right[:, at : at + chunk])
            ds_ref[:, at : at + chunk] = (
                p_ref[:, at : at + chunk].astype(f32) * grad_probs
            ).astype(bf16)
        grad_scores = ds_ref[...]
        turned_grad = dot(turned(keys), grad_scores)
        dq_ref[...] = (
            turned(
                jnp.concatenate([turned_grad[:half, :tokens], turned_grad[half:, tokens:]], axis=0)
            )
            * scale
        ).astype(bf16)
        grad_keys = dot(grad_scores, head_blocks(q_ref[...])).astype(bf16)
        grad_values = dot_rows(p_ref[...], scaled).astype(bf16)
        at = 0
        for i, part in enumerate(parts):
            rows = part.shape[0]
            dkv_refs[2 * i][...] = grad_keys[at : at + rows]
            dkv_refs[2 * i + 1][...] = grad_values[at : at + rows]
            at += rows

    sources = [query, grad_mixed, mixed_t, weights, inverse]
    out_shapes = [shape(tokens, width, bf16)]
    columns = lambda p, s: (0, p)
    out_specs = [pl.BlockSpec((tokens, LANES), columns)]
    for part in parts:
        sources += [part, part]
        rows = part.shape[0]
        out_shapes += [shape(rows, width, bf16)] * 2
        out_specs += [pl.BlockSpec((rows, LANES), columns)] * 2
    return pl.pallas_call(
        body,
        name="attend_back",
        out_shape=out_shapes,
        grid_spec=pltpu.PrefetchScalarGridSpec(
            num_scalar_prefetch=1,
            grid=(pairs,),
            in_specs=[
                pl.BlockSpec((tokens, LANES), columns),
                pl.BlockSpec((tokens, LANES), columns),
                pl.BlockSpec((LANES, tokens), lambda p, s: (p, 0)),
                pl.BlockSpec((None, span, 2 * tokens), lambda p, s: (p, 0, 0)),
                pl.BlockSpec((None, 1, 2 * tokens), lambda p, s: (p, 0, 0)),
            ]
            + pair_specs(parts, pairs),
            out_specs=out_specs,
            scratch_shapes=[pltpu.VMEM((span, 2 * tokens), bf16)],
        ),
        compiler_params=pltpu.CompilerParams(vmem_limit_bytes=56 << 20),
    )(jnp.zeros((1,), jnp.int32), *sources)


def normalize(resid):
    center = resid - jnp.mean(resid, axis=1, keepdims=True)
    inverse = lax.rsqrt(jnp.mean(center * center, axis=1, keepdims=True) + norm_eps)
    return center * inverse, inverse


def norm_back(grads, normal, inverse, gain):
    scaled = grads * gain
    return inverse * (
        scaled
        - jnp.mean(scaled, axis=1, keepdims=True)
        - normal * jnp.mean(scaled * normal, axis=1, keepdims=True)
    )


def column_sums(value):
    return jnp.sum(value, axis=0, keepdims=True)


def masked_total(value, valid, width):
    lanes = column_sums(jnp.where(valid, value * value, 0.0))
    return jnp.broadcast_to(jnp.sum(lanes, axis=1, keepdims=True), (1, width))


def valid_rows(scalar, at, tokens):
    position = scalar[at + 1] + lax.broadcasted_iota(jnp.int32, (tokens, 1), 0)
    return position < scalar[at]


def after_attention(links, table, rows, mixed, vectors, mine, theirs, out_piece):
    tokens, width = rows.shape
    extra = 4 * links.dp + 1

    def body(scalar, rows_ref, mixed_ref, vec_ref, mine_ref, theirs_ref, *refs):
        hidden_ref, low_ref, normal_ref, inverse_ref, sums_ref, weight, sem = refs
        out_piece.fetch(scalar, (mine_ref, theirs_ref), weight, sem.at[0])
        x = rows_ref[...].astype(f32)
        valid = valid_rows(scalar, extra, tokens)
        sums_ref[0:1, :] = masked_total(x, valid, width)
        count = jnp.sum(valid.astype(f32), axis=0, keepdims=True)
        sums_ref[2:3, :] = jnp.broadcast_to(count, (1, width))
        out_piece.ready(weight, sem.at[0])
        branch = dot(mixed_ref[...], weight[...]) + vec_ref[2:3]
        sums_ref[1:2, :] = masked_total(branch, valid, width)
        normal, inverse = normalize(x + branch)
        hidden = normal * vec_ref[3:4] + vec_ref[4:5]
        normal_ref[...] = normal
        inverse_ref[...] = inverse
        hidden_ref[...] = hidden
        low_ref[...] = hidden.astype(bf16)

    return call(
        body,
        "after_attention",
        [table, rows, mixed, vectors, mine, theirs],
        [SMEM, VMEM, VMEM, VMEM, ANY, ANY],
        [
            shape(tokens, width, f32),
            shape(tokens, width, bf16),
            shape(tokens, width, f32),
            shape(tokens, 1, f32),
            shape(3, width, f32),
        ],
        [out_piece.whole(), pltpu.SemaphoreType.DMA((1,))],
    )


def gelu_and_slope(u):
    size = jnp.abs(u)
    t = 1.0 / (1.0 + (0.3275911 * math.sqrt(0.5)) * size)
    bell = jnp.exp(-0.5 * (u * u))
    series = 0.5 * 1.061405429 * t - 0.5 * 1.453152027
    series = series * t + 0.5 * 1.421413741
    series = series * t - 0.5 * 0.284496736
    series = series * t + 0.5 * 0.254829592
    tail = series * t * bell
    phi = jnp.where(u < 0.0, tail, 1.0 - tail)
    return u * phi, phi + u * bell * (1.0 / math.sqrt(2.0 * math.pi))


def feed_forward(links, table, hidden, low, vectors, up_bias, cotangent, up, down, pieces):
    tokens, width = hidden.shape
    up_piece, down_piece = pieces
    inner = up_bias.shape[1]
    block = width
    extra = 4 * links.dp + 1
    dp = links.dp

    def body(scalar, hidden_ref, low_ref, vec_ref, bias_ref, cot_ref, um, ut, dm, dt, *refs):
        out_ref, slope_ref, resid_ref, grad_ref, keep_ref, send_ref, sums_ref = refs[:7]
        up_w, down_w, act, total, tile, sems = refs[7:]
        up_piece.fetch(scalar, (um, ut), up_w, sems.at[0])
        down_piece.fetch(scalar, (dm, dt), down_w, sems.at[1])
        up_piece.ready(up_w, sems.at[0])
        down_piece.ready(down_w, sems.at[1])
        total[...] = jnp.zeros_like(total)

        def forward(j, carry):
            at = aligned(j * block, block, LANES)
            u = dot(low_ref[...], up_w[:, at]) + bias_ref[:, at]
            value, slope = gelu_and_slope(u)
            value = value.astype(bf16)
            act[:, at] = value
            slope_ref[:, at] = slope.astype(bf16)
            total[...] += dot(value, down_w[at, :])
            return carry

        lax.fori_loop(0, inner // block, forward, 0)
        branch = total[...] + vec_ref[5:6]
        sums_ref[3:4, :] = masked_total(branch, valid_rows(scalar, extra, tokens), width)
        normal, inverse = normalize(hidden_ref[...] + branch)
        out_ref[...] = (normal * vec_ref[6:7] + vec_ref[7:8]).astype(bf16)
        grads = cot_ref[...].astype(f32)
        sums_ref[1:2, :] = column_sums(grads * normal)
        sums_ref[2:3, :] = column_sums(grads)
        resid = norm_back(grads, normal, inverse, vec_ref[6:7])
        resid_ref[...] = resid
        grad_ffn = resid.astype(bf16)
        grad_ref[...] = grad_ffn
        sums_ref[0:1, :] = column_sums(grad_ffn.astype(f32))
        core = scalar[4 * dp]

        def backward(j, carry):
            at = aligned(j * block, block, LANES)
            tile[...] = dot(turned(act[:, at]), grad_ref[...])
            for side, out in enumerate((keep_ref, send_ref)):
                half = core if side == 0 else 1 - core
                spread(
                    scalar,
                    dp,
                    side,
                    tile,
                    out,
                    down_piece.rows,
                    slice(None),
                    aligned(half * down_piece.columns, down_piece.columns, LANES),
                    j * (block // down_piece.rows),
                )
            return carry

        lax.fori_loop(0, inner // block, backward, 0)

    return call(
        body,
        "feed_forward",
        [table, hidden, low, vectors, up_bias, cotangent, *up, *down],
        [SMEM] + [VMEM] * 5 + [ANY] * 4,
        [
            shape(tokens, width, bf16),
            shape(tokens, inner, bf16),
            shape(tokens, width, f32),
            shape(tokens, width, bf16),
            shape(inner, width // 2, bf16),
            shape(inner, width // 2, bf16),
            shape(4, width, f32),
        ],
        [
            up_piece.whole(),
            down_piece.whole(),
            pltpu.VMEM((tokens, inner), bf16),
            pltpu.VMEM((tokens, width), f32),
            pltpu.VMEM((block, width), f32),
            pltpu.SemaphoreType.DMA((2,)),
        ],
    )


def feed_back(links, table, low, slope, resid, grad_ffn, up, down, pieces):
    tokens, width = resid.shape
    up_piece, down_piece = pieces
    inner = slope.shape[1]
    span = inner // 2
    block = width if span % width == 0 else span
    dp = links.dp

    def body(scalar, low_ref, slope_ref, resid_ref, grad_ref, um, ut, dm, dt, *refs):
        hidden_ref, keep_ref, send_ref, bias_ref, up_w, down_w, low_t, tile, sems = refs
        up_piece.fetch(scalar, (um, ut), up_w, sems.at[0])
        down_piece.fetch(scalar, (dm, dt), down_w, sems.at[1])
        low_t[...] = turned(low_ref[...])
        hidden_ref[...] = resid_ref[...]
        up_piece.ready(up_w, sems.at[0])
        down_piece.ready(down_w, sems.at[1])
        core = scalar[4 * dp]
        for side, out in enumerate((keep_ref, send_ref)):
            half = core if side == 0 else 1 - core

            def backward(j, carry, side=side, out=out, half=half):
                at = aligned(half * span + j * block, block, LANES)
                grads = dot_rows(grad_ref[...], down_w[at, :]) * slope_ref[:, at].astype(f32)
                grads = grads.astype(bf16)
                bias_ref[:, at] = column_sums(grads.astype(f32))
                hidden_ref[...] += dot_rows(grads, up_w[:, at])
                tile[...] = dot(low_t[...], grads)
                spread(
                    scalar,
                    dp,
                    side,
                    tile,
                    out,
                    up_piece.rows,
                    aligned(j * block, block, LANES),
                    slice(None),
                    0,
                )
                return carry

            lax.fori_loop(0, span // block, backward, 0)

    return call(
        body,
        "feed_back",
        [table, low, slope, resid, grad_ffn, *up, *down],
        [SMEM] + [VMEM] * 4 + [ANY] * 4,
        [
            shape(tokens, width, f32),
            shape(width, span, bf16),
            shape(width, span, bf16),
            shape(1, inner, f32),
        ],
        [
            up_piece.whole(),
            down_piece.whole(),
            pltpu.VMEM((width, tokens), bf16),
            pltpu.VMEM((width, block), f32),
            pltpu.SemaphoreType.DMA((2,)),
        ],
    )


def before_attention(links, table, grad_hidden, normal, inverse, mixed, vectors, attn, piece):
    tokens, width = normal.shape

    def body(scalar, grad_ref, normal_ref, inverse_ref, mixed_ref, vec_ref, mine, theirs, *refs):
        resid_ref, gm_ref, out_ref, sums_ref, weight, sem = refs
        piece.fetch(scalar, (mine, theirs), weight, sem.at[0])
        grads = grad_ref[...]
        normal_ = normal_ref[...]
        sums_ref[1:2, :] = column_sums(grads * normal_)
        sums_ref[2:3, :] = column_sums(grads)
        resid = norm_back(grads, normal_, inverse_ref[...], vec_ref[3:4])
        resid_ref[...] = resid
        grad_attn = resid.astype(bf16)
        sums_ref[0:1, :] = column_sums(grad_attn.astype(f32))
        piece.ready(weight, sem.at[0])
        gm_ref[...] = dot_rows(grad_attn, weight[...]).astype(bf16)
        out_ref[...] = dot(turned(mixed_ref[...]), grad_attn).astype(bf16)

    return call(
        body,
        "before_attention",
        [table, grad_hidden, normal, inverse, mixed, vectors, *attn],
        [SMEM] + [VMEM] * 5 + [ANY] * 2,
        [
            shape(tokens, width, f32),
            shape(tokens, width, bf16),
            shape(width, width, bf16),
            shape(3, width, f32),
        ],
        [piece.whole(), pltpu.SemaphoreType.DMA((1,))],
    )


def qkv_gradient(links, table, rows, query_grad, mine, theirs, out_grad, vectors, pieces):
    tokens, width = rows.shape
    qkv_piece, out_piece, vector_piece = pieces
    dp = links.dp
    count = 2 if theirs else 1
    total = qkv_piece.columns + out_piece.columns + LANES

    def body(scalar, rows_ref, dq_ref, *refs):
        share_refs = refs[: 2 * count]
        out_ref, vec_ref, grads_ref, keep_ref, send_ref, tile, vec_tile = refs[2 * count :]
        grads_ref[:, :width] = dq_ref[...]
        for i in range(2):
            share = share_refs[i][...]
            if count == 2:
                share = (share.astype(f32) + share_refs[2 + i][...].astype(f32)).astype(bf16)
            grads_ref[:, (1 + i) * width : (2 + i) * width] = share
        rows_t = turned(rows_ref[...])
        for i in range(3):
            at = slice(i * width, (i + 1) * width)
            tile[:, at] = dot(rows_t, grads_ref[:, at]).astype(bf16)
        sums = vec_ref[...]
        query_sum = column_sums(grads_ref[:, :width].astype(f32))
        value_sum = column_sums(grads_ref[:, 2 * width :].astype(f32))
        row = lax.broadcasted_iota(jnp.int32, (LANES, width), 0)
        padded = jnp.concatenate([sums, jnp.zeros((LANES - VECTORS, width), f32)], axis=0)
        padded = jnp.where(row == 0, query_sum, jnp.where(row == 1, value_sum, padded))
        vec_tile[...] = turned(padded).astype(bf16)
        core = scalar[4 * dp]
        for side, out in enumerate((keep_ref, send_ref)):
            half = core if side == 0 else 1 - core
            for source, piece in ((tile, qkv_piece), (out_ref, out_piece), (vec_tile, vector_piece)):
                columns = (
                    slice(None)
                    if piece is vector_piece
                    else aligned(half * piece.columns, piece.columns, LANES)
                )
                spread(
                    scalar,
                    dp,
                    side,
                    source,
                    out,
                    piece.rows,
                    slice(piece.first, piece.first + piece.columns),
                    columns,
                    0,
                )

    return call(
        body,
        "qkv_gradient",
        [table, rows, query_grad, *mine, *theirs, out_grad, vectors],
        [SMEM] + [VMEM] * (4 + 2 * count),
        [
            shape(tokens, 3 * width, bf16),
            shape(width, total, bf16),
            shape(width, total, bf16),
        ],
        [pltpu.VMEM((width, 3 * width), bf16), pltpu.VMEM((width, LANES), bf16)],
    )


def input_gradient(links, table, grads, resid, attn, qkv_piece):
    tokens, width = resid.shape

    def body(scalar, grads_ref, resid_ref, mine, theirs, out_ref, weight, sem):
        qkv_piece.fetch(scalar, (mine, theirs), weight, sem.at[0])
        qkv_piece.ready(weight, sem.at[0])
        out_ref[...] = resid_ref[...] + dot_rows(grads_ref[...], weight[...])

    return call(
        body,
        "input_gradient",
        [table, grads, resid, *attn],
        [SMEM, VMEM, VMEM, ANY, ANY],
        [shape(tokens, width, f32)],
        [qkv_piece.whole(), pltpu.SemaphoreType.DMA((1,))],
    )[0]


def settle(links, kept, sent, pieces):
    mine = links.reduce(kept, links.swap(sent))
    theirs = links.swap(mine)
    return [
        both_halves(
            links,
            mine[:, piece.first : piece.first + piece.columns],
            theirs[:, piece.first : piece.first + piece.columns],
        )
        for piece in pieces
    ]


def shards(
    tokens,
    lengths,
    qkv_weight,
    query_bias,
    value_bias,
    out_weight,
    out_bias,
    norm1_gain,
    norm1_shift,
    up_weight,
    up_bias,
    down_weight,
    down_bias,
    norm2_gain,
    norm2_shift,
    cotangent,
):
    seq_dev, ctx_tok, width = tokens.shape
    assert seq_dev == 1 and width // HEADS == LANES // 2
    scale = (width // HEADS) ** (-0.5)
    links = Links()
    dp = links.dp
    rows = tokens.reshape(ctx_tok, width)
    cot = cotangent.reshape(ctx_tok, width)
    block = lax.axis_index("ctx")
    start = block * ctx_tok
    table = links.table(lengths[0], start)

    shard = qkv_weight.shape[0]
    inner = down_weight.shape[0] * dp
    folds = down_weight.shape[0] // shard
    half = [w.shape[1] // 2 for w in (qkv_weight, out_weight, up_weight, down_weight)]
    qkv_piece = Piece(dp, shard, half[0], 0)
    out_piece = Piece(dp, shard, half[1], half[0])
    vector_piece = Piece(dp, shard, LANES, half[0] + half[1])
    up_piece = Piece(dp, shard, half[2], 0)
    down_piece = Piece(dp, down_weight.shape[0], half[3], 0)

    columns = [query_bias, value_bias, out_bias, norm1_gain, norm1_shift]
    columns += [down_bias, norm2_gain, norm2_shift]
    base = len(columns)
    columns += [up_bias[i * shard : (i + 1) * shard] for i in range(folds)]
    packed = jnp.stack(columns, axis=1)
    packed = jnp.pad(packed, ((0, 0), (0, LANES - packed.shape[1])))
    attn_piece = jnp.concatenate(
        [half_columns(links, qkv_weight), half_columns(links, out_weight), packed], axis=1
    )
    attn_mine = links.gather(attn_piece)
    attn = (attn_mine, links.swap(attn_mine))
    up_mine = links.gather(half_columns(links, up_weight))
    up = (up_mine, links.swap(up_mine))
    down_mine = links.gather(half_columns(links, down_weight))
    down = (down_mine, links.swap(down_mine))

    query, kv, vectors = project(
        links, table, rows, *attn, qkv_piece, vector_piece, scale
    )
    up_bias_row = (
        vectors[base : base + folds].reshape(folds, dp, shard).transpose(1, 0, 2).reshape(1, inner)
    )
    if links.ctx == 2:
        parts = [kv, links.swap(kv)]
        starts = [start, (1 - block) * ctx_tok]
    else:
        parts = [lax.all_gather(kv, "ctx", axis=0, tiled=True)]
        starts = [jnp.int32(0)]
    mixed_t, mixed, weights, inverse = attend(query, parts, starts, lengths[0])
    hidden, low, normal, deviation, sums1 = after_attention(
        links, table, rows, mixed, vectors, *attn, out_piece
    )
    output, slope, resid2, grad_ffn, down_keep, down_send, sums2 = feed_forward(
        links, table, hidden, low, vectors, up_bias_row, cot, up, down, (up_piece, down_piece)
    )
    (down_grad,) = settle(links, down_keep, down_send, [down_piece])
    grad_hidden, up_keep, up_send, up_bias_grad = feed_back(
        links, table, low, slope, resid2, grad_ffn, up, down, (up_piece, down_piece)
    )
    (up_grad,) = settle(links, up_keep, up_send, [up_piece])
    resid1, grad_mixed, out_grad, sums3 = before_attention(
        links, table, grad_hidden, normal, deviation, mixed, vectors, attn, out_piece
    )
    back = attend_back(query, parts, grad_mixed, mixed_t, weights, inverse, scale)
    if links.ctx == 2:
        received = links.swap(jnp.concatenate([back[3], back[4]], axis=1))
        mine, theirs = back[1:3], [received[:, :width], received[:, width:]]
    else:
        both = lax.psum_scatter(
            jnp.concatenate(back[1:3], axis=1), "ctx", scatter_dimension=0, tiled=True
        )
        mine, theirs = [both[:, :width], both[:, width:]], []
    up_bias_rows = (
        up_bias_grad.reshape(dp, folds, shard).transpose(1, 0, 2).reshape(folds, width)
    )
    blank = jnp.zeros((2, width), f32)
    sent = jnp.concatenate([blank, sums3, sums2[0:3], up_bias_rows, sums1, sums2[3:4]], axis=0)
    sent = jnp.pad(sent, ((0, VECTORS - sent.shape[0]), (0, 0)))
    grads, attn_keep, attn_send = qkv_gradient(
        links,
        table,
        rows,
        back[0],
        list(mine),
        list(theirs),
        out_grad,
        sent,
        (qkv_piece, out_piece, vector_piece),
    )
    qkv_grad, out_grad, vector_grad = settle(
        links, attn_keep, attn_send, [qkv_piece, out_piece, vector_piece]
    )
    input_grad = input_gradient(links, table, grads, resid1, attn, qkv_piece)
    sums = jnp.transpose(vector_grad[:, :LANES])
    at = base + folds
    stream = sums[at : at + 4, 0]
    stream_rms = jnp.sqrt(
        jnp.stack([stream[0], stream[1], stream[3]]) / (stream[2] * width) + 1e-06
    )
    return (
        output.reshape(seq_dev, ctx_tok, width),
        input_grad.reshape(seq_dev, ctx_tok, width),
        stream_rms,
        qkv_grad,
        sums[0],
        sums[1],
        out_grad,
        sums[2],
        sums[3],
        sums[4],
        up_grad,
        sums[base : base + folds].reshape(-1),
        down_grad,
        sums[5],
        sums[6],
        sums[7],
    )


def solution(mesh):
    in_specs = (
        P("dp", "ctx", None),
        P("dp"),
        P("dp", None),
        P("dp"),
        P("dp"),
        P("dp", None),
        P("dp"),
        P("dp"),
        P("dp"),
        P("dp", None),
        P("dp"),
        P("dp", None),
        P("dp"),
        P("dp"),
        P("dp"),
        P("dp", "ctx", None),
    )
    out_specs = (
        P("dp", "ctx", None),
        P("dp", "ctx", None),
        P(),
        P("dp", None),
        P("dp"),
        P("dp"),
        P("dp", None),
        P("dp"),
        P("dp"),
        P("dp"),
        P("dp", None),
        P("dp"),
        P("dp", None),
        P("dp"),
        P("dp"),
        P("dp"),
    )
    return jax.shard_map(shards, mesh=mesh, in_specs=in_specs, out_specs=out_specs, check_vma=False)
```

time: 448 us -> 353 us (0.79); the launches traced: 440 us -> 351 us
  matrix products: 128 us -> 0 us
  Pallas kernels: 28.1 us -> 118 us
  local copies, waits for them, and re-layouts: 61.7 us -> 26.1 us
  waiting for transfers between devices: 92.4 us -> 123 us
  other arithmetic: 53.7 us -> 29.8 us
  starting transfers between devices: 71.7 us -> 51.9 us
    dot_general x26 -> x0, matrix products: 128 us -> none  [the longest x4 29.3 us: matmul(): return jnp.dot(left, right, preferred_element_type=jnp.float32)]
    pallas_call x6 -> x9, Pallas kernels: 28.1 us -> 118 us  [the longest x7 80.1 us: call(): pl.pallas_call(body, name=name, out_shape=outs, in_specs=in_specs, out_sp...]
    ppermute x30, waiting for transfers between devices: 91.9 us -> 121 us  [hop(): return lax.ppermute(value, ('ctx', 'dp'), pairs)]
    ppermute x30, starting transfers between devices: 69.5 us -> 49.8 us  [hop(): return lax.ppermute(value, ('ctx', 'dp'), pairs)]
    reduce_sum x14 -> x0, other arithmetic: 13.1 us -> none  [the longest x2 5.2 us: first_sweep(): jnp.sum(jnp.exp(scores - new_max[..., None]), axis=-1)]
    dynamic_slice x8 -> x0, local copies, waits for them, and re-layouts: 11.9 us -> none  [head_slice(): piece = lax.dynamic_slice_in_dim(source, key_start, key_span, 0)]
    another operation x11 -> x3, local copies, waits for them, and re-layouts: 9.57 us -> 1.81 us  [shards(): packed = jnp.stack(columns, axis=1)]
    select_n x3 -> x0, other arithmetic: 5.59 us -> none  [the longest x1 3.59 us: own_block(): theirs = links.swap(jnp.where(even, second, first))]
  transfers between devices with their start and end apart: 41 -> 41, of which waited for: 15 -> 18; matrix products, arithmetic and copies ran while one was open for 19% -> 13% of each run, Pallas kernels for 6% -> 26%
where the time goes in v2:
time: 353 us; the launch traced here: 351 us
  waiting for transfers between devices  123 us (35%)
  Pallas kernels  118 us (33%)
  starting transfers between devices  51.9 us (15%)
  other arithmetic  29.8 us (8%)
  local copies, waits for them, and re-layouts  26.1 us (7%)
    ppermute x30, waiting for transfers between devices, hop(): return lax.ppermute(value, ('ctx', 'dp'), pairs)  121 us
    pallas_call x7, Pallas kernels, call(): pl.pallas_call(body, name=name, out_shape=outs, in_specs=in_specs, out_sp...  80.1 us
    ppermute x30, starting transfers between devices, hop(): return lax.ppermute(value, ('ctx', 'dp'), pairs)  49.8 us
    pallas_call x1, Pallas kernels, attend(): pl.pallas_call(body, name='attend', out_shape=[shape(width, tokens, f32),...  21.6 us
    convert_element_type x12, other arithmetic, total(): return value.astype(bf16)  19.4 us
    pallas_call x1, Pallas kernels, attend_back(): pl.pallas_call(body, name='attend_back', out_shape=out_shapes, grid_spec=...  15.9 us
    unnamed x45, local copies, waits for them, and re-layouts  11.2 us
  transfers between devices with their start and end apart: 41, of which 18 were waited for; matrix products, arithmetic and copies ran while one was open for 13% of the time, Pallas kernels for 26%

profile of v2, /device:TPU:0, one launch (start us, length us, event | category | flops | bytes accessed | tf_op | source)
XLA Modules:
  0.0 351.2 jit_solution(10549573244707186070)
XLA Ops:
  2.3 3.0 collective-permute-start.13
  12.2 3.5 collective-permute-start.1
  19.5 11.3 %collective-permute-start.8 = (bf16[48,1536]{1,0:T(8,128)(2,1)S(1)}, bf16[48,1536]{1,0:T(8,128)(2,1)S(1)}, u32[]{:S(2)}, u32[]{:S(2)}) collective-permute-start(bf16[48,1536]{1,0:T(8,128)(2,1)S(1)} %get-tuple-element.97), channel_id=1, source_target_pairs={{0,8},{1,9},{2,10},{3,11},{4,12},{5,13},{6,14},{7,15},{8,0},{9,1},... | collective-permute-start | bytes 442376 | tf_op jit(solution)/shard_map/ppermute | solution.py:46
  33.4 5.7 %collective-permute-done.1 = bf16[48,1664]{1,0:T(8,128)(2,1)S(1)} collective-permute-done((bf16[48,1664]{1,0:T(8,128)(2,1)}, bf16[48,1664]{1,0:T(8,128)(2,1)S(1)}, u32[]{:S(2)}, u32[]{:S(2)}) %collective-permute-start.1) | collective-permute-done | bytes 159776 | tf_op jit(solution)/shard_map/ppermute | solution.py:46
  41.4 21.5 %collective-permute-done.3 = bf16[192,1664]{1,0:T(8,128)(2,1)S(1)} collective-permute-done((bf16[192,1664]{1,0:T(8,128)(2,1)S(1)}, bf16[192,1664]{1,0:T(8,128)(2,1)S(1)}, u32[]{:S(2)}, u32[]{:S(2)}) %collective-permute-start.3) | collective-permute-done | bytes 639008 | tf_op jit(solution)/shard_map/ppermute | solution.py:46
  72.2 8.2 %collective-permute-done.4 = bf16[384,1664]{1,0:T(8,128)(2,1)S(1)} collective-permute-done((bf16[384,1664]{1,0:T(8,128)(2,1)S(1)}, bf16[384,1664]{1,0:T(8,128)(2,1)S(1)}, u32[]{:S(2)}, u32[]{:S(2)}) %collective-permute-start.4) | collective-permute-done | bytes 1277984 | tf_op jit(solution)/shard_map/ppermute | solution.py:46
  84.7 13.3 %collective-permute-done.17 = bf16[1536,384]{1,0:T(8,128)(2,1)S(1)} collective-permute-done((bf16[1536,384]{1,0:T(8,128)(2,1)S(1)}, bf16[1536,384]{1,0:T(8,128)(2,1)S(1)}, u32[]{:S(2)}, u32[]{:S(2)}) %collective-permute-start.17) | collective-permute-done | bytes 1179680 | tf_op jit(solution)/shard_map/ppermute | solution.py:46
  99.1 11.5 %collective-permute-done.11 = bf16[384,1536]{1,0:T(8,128)(2,1)S(1)} collective-permute-done((bf16[384,1536]{1,0:T(8,128)(2,1)S(1)}, bf16[384,1536]{1,0:T(8,128)(2,1)S(1)}, u32[]{:S(2)}, u32[]{:S(2)}) %collective-permute-start.11) | collective-permute-done | bytes 1179680 | tf_op jit(solution)/shard_map/ppermute | solution.py:46
  113.1 6.6 %qkv.1 = (bf16[512,768]{1,0:T(8,128)(2,1)}, bf16[512,1536]{1,0:T(8,128)(2,1)}, f32[16,768]{1,0:T(8,128)}) custom-call(s32[67]{0:T(128)} %concatenate.61.scalar, bf16[512,768]{1,0:T(8,128)(2,1)} %bitcast.36, bf16[768,1664]{1,0:T(8,128)(2,1)} %copy-done.2, bf16[768,1664]{1,0:T(8,128)(2,1)} %collective-permute-done.5.theirs_ref.theirs), custom_call_target="tpu_custom_call" | custom-call | tf_op jit(solution)/shard_map/qkv/pallas_call | solution.py:152
  124.7 21.6 %attend.1 = (f32[768,512]{1,0:T(8,128)}, bf16[512,768]{1,0:T(8,128)(2,1)}, bf16[6,1024,1024]{2,1,0:T(8,128)(2,1)}, f32[6,1,1024]{2,1,0:T(1,128)}) custom-call(s32[3]{0:T(128)} %pad_add_fusion.scalar, bf16[512,768]{1,0:T(8,128)(2,1)} %get-tuple-element.51.q_ref, bf16[512,1536]{1,0:T(8,128)(2,1)} %get-tuple-element.52.refs_0_.refs_1_, ...), custom_call_target="tpu_custom_call" | custom-call | tf_op jit(solution)/shard_map/attend/pallas_call | solution.py:323
  146.3 6.1 %after_attention.1 = (f32[512,768]{1,0:T(8,128)}, bf16[512,768]{1,0:T(8,128)(2,1)}, f32[512,768]{1,0:T(8,128)}, f32[512,1]{1,0:T(8,128)}, f32[3,768]{1,0:T(4,128)}) custom-call(s32[67]{0:T(128)} %concatenate.61.scalar, bf16[512,768]{1,0:T(8,128)(2,1)} %bitcast.37, bf16[512,768]{1,0:T(8,128)(2,1)} %get-tuple-element.53.mixed_ref, ...), custom_call_target="tpu_custom_call" | custom-call | tf_op jit(solution)/shard_map/after_attention/pallas_call | solution.py:152
  152.4 26.1 %feed_forward.1 = (bf16[512,768]{1,0:T(8,128)(2,1)}, bf16[512,3072]{1,0:T(8,128)(2,1)}, f32[512,768]{1,0:T(8,128)}, bf16[512,768]{1,0:T(8,128)(2,1)}, bf16[3072,...) custom-call(s32[67]{0:T(128)} %concatenate.61.scalar, f32[512,768]{1,0:T(8,128)} %get-tuple-element.55.hidden_ref, ...), custom_call_target="tpu_custom_call" | custom-call | tf_op jit(solution)/shard_map/feed_forward/pallas_call | solution.py:152
  178.9 18.9 %feed_back.1 = (f32[512,768]{1,0:T(8,128)}, bf16[768,1536]{1,0:T(8,128)(2,1)}, bf16[768,1536]{1,0:T(8,128)(2,1)}, f32[1,3072]{1,0:T(1,128)}) custom-call(s32[67]{0:T(128)} %concatenate.61.scalar, bf16[512,768]{1,0:T(8,128)(2,1)} %get-tuple-element.56.low_ref, bf16[512,3072]{1,0:T(8,128)(2,1)} %get-tuple-element.58.slope_ref, ...), custom_call_target="tpu_custom_call" | custom-call | tf_op jit(solution)/shard_map/feed_back/pallas_call | solution.py:152
  197.8 5.9 %before_attention.1 = (f32[512,768]{1,0:T(8,128)}, bf16[512,768]{1,0:T(8,128)(2,1)}, bf16[768,768]{1,0:T(8,128)(2,1)}, f32[3,768]{1,0:T(4,128)}) custom-call(s32[67]{0:T(128)} %concatenate.61.scalar, f32[512,768]{1,0:T(8,128)} %get-tuple-element.61.grad_ref, f32[512,768]{1,0:T(8,128)} %get-tuple-element.62.normal_ref, ...), custom_call_target="tpu_custom_call" | custom-call | tf_op jit(solution)/shard_map/before_attention/pallas_call | solution.py:152
  203.7 15.9 %attend_back.1 = (bf16[512,768]{1,0:T(8,128)(2,1)}, bf16[512,768]{1,0:T(8,128)(2,1)}, bf16[512,768]{1,0:T(8,128)(2,1)}, bf16[512,768]{1,0:T(8,128)(2,1)}, bf16[512,768]{1,0:T(8,128)(2,1)}) custom-call(s32[1]{0:T(128)} %constant.139.clone.1._, bf16[512,768]{1,0:T(8,128)(2,1)} %get-tuple-element.51.q_ref, bf16[512,768]{1,0:T(8,128)(2,1)} %get-tuple-element.64.gm_ref, ...), custom_call_target="tpu_custom_call" | custom-call | tf_op jit(solution)/shard_map/attend_back/pallas_call | solution.py:418
  226.9 9.2 %qkv_gradient.1 = (bf16[512,2304]{1,0:T(8,128)(2,1)}, bf16[768,1664]{1,0:T(8,128)(2,1)}, bf16[768,1664]{1,0:T(8,128)(2,1)}) custom-call(s32[67]{0:T(128)} %concatenate.61.scalar, bf16[512,768]{1,0:T(8,128)(2,1)} %bitcast.38, bf16[512,768]{1,0:T(8,128)(2,1)} %get-tuple-element.68.dq_ref, bf16[512,768]{1,0:T(8,128)(2,1)} %get-tuple-element.69.refs_0_, ...), custom_call_target="tpu_custom_call" | custom-call | tf_op jit(solution)/shard_map/qkv_gradient/pallas_call | solution.py:152
  241.7 12.5 %collective-permute-done.35 = bf16[1536,384]{1,0:T(8,128)(2,1)S(1)} collective-permute-done((bf16[1536,384]{1,0:T(8,128)(2,1)S(1)}, bf16[1536,384]{1,0:T(8,128)(2,1)S(1)}, u32[]{:S(2)}, u32[]{:S(2)}) %collective-permute-start.35) | collective-permute-done | bytes 1179680 | tf_op jit(solution)/shard_map/ppermute | solution.py:46
  258.5 14.7 %collective-permute-done.28 = bf16[384,1536]{1,0:T(8,128)(2,1)S(1)} collective-permute-done((bf16[384,1536]{1,0:T(8,128)(2,1)S(1)}, bf16[384,1536]{1,0:T(8,128)(2,1)S(1)}, u32[]{:S(2)}, u32[]{:S(2)}) %collective-permute-start.28) | collective-permute-done | bytes 1179680 | tf_op jit(solution)/shard_map/ppermute | solution.py:46
  280.2 7.4 %input_gradient.1 = f32[512,768]{1,0:T(8,128)} custom-call(s32[67]{0:T(128)} %concatenate.61.scalar, bf16[512,2304]{1,0:T(8,128)(2,1)} %get-tuple-element.78.grads_ref, f32[512,768]{1,0:T(8,128)} %get-tuple-element.79.resid_ref, bf16[768,1664]{1,0:T(8,128)(2,1)} %copy-done.2, bf16[768,1664]{1,0:T(8,128)(2,1)} %collective-permute-done.5.theirs_ref.theirs), custom_call_target="tpu_custom_call" | custom-call | tf_op jit(solution)/shard_map/input_gradient/pallas_call | solution.py:152
  287.6 4.4 %collective-permute-done.29 = bf16[192,1536]{1,0:T(8,128)(2,1)} collective-permute-done((bf16[192,1536]{1,0:T(8,128)(2,1)}, bf16[192,1536]{1,0:T(8,128)(2,1)}, u32[]{:S(2)}, u32[]{:S(2)}) %collective-permute-start.29) | collective-permute-done | bytes 589856 | tf_op jit(solution)/shard_map/ppermute | solution.py:46
  295.5 2.7 collective-permute-start.32
  301.3 8.0 %collective-permute-done.31 = bf16[48,1536]{1,0:T(8,128)(2,1)S(1)} collective-permute-done((bf16[48,1536]{1,0:T(8,128)(2,1)S(1)}, bf16[48,1536]{1,0:T(8,128)(2,1)S(1)}, u32[]{:S(2)}, u32[]{:S(2)}) %collective-permute-start.31) | collective-permute-done | bytes 147488 | tf_op jit(solution)/shard_map/ppermute | solution.py:46
  317.6 6.2 %collective-permute-done.22 = bf16[192,1664]{1,0:T(8,128)(2,1)S(1)} collective-permute-done((bf16[192,1664]{1,0:T(8,128)(2,1)S(1)}, bf16[192,1664]{1,0:T(8,128)(2,1)S(1)}, u32[]{:S(2)}, u32[]{:S(2)}) %collective-permute-start.22) | collective-permute-done | bytes 639008 | tf_op jit(solution)/shard_map/ppermute | solution.py:46
  333.0 8.7 %collective-permute-done.24 = bf16[48,1664]{1,0:T(8,128)(2,1)S(1)} collective-permute-done((bf16[48,1664]{1,0:T(8,128)(2,1)S(1)}, bf16[48,1664]{1,0:T(8,128)(2,1)S(1)}, u32[]{:S(2)}, u32[]{:S(2)}) %collective-permute-start.24) | collective-permute-done | bytes 159776 | tf_op jit(solution)/shard_map/ppermute | solution.py:46
  (173 shorter events, 95.9 us)
Async XLA Ops:
  11.3 20.5 %collective-permute-start = (bf16[48,1664]{1,0:T(8,128)(2,1)}, bf16[48,1664]{1,0:T(8,128)(2,1)S(1)}, u32[]{:S(2)}, u32[]{:S(2)}) collective-permute-start(bf16[48,1664]{1,0:T(8,128)(2,1)} %get-tuple-element.131), channel_id=1, source_target_pairs={{0,4},{1,5},{2,6},{3,7},{4,0},{5,1},{6,2},{7,3},{8,12},{9,13},{10,... | collective-permute-start | bytes 479240 | tf_op jit(solution)/shard_map/ppermute | solution.py:46
  12.2 26.9 %collective-permute-start.1 = (bf16[48,1664]{1,0:T(8,128)(2,1)}, bf16[48,1664]{1,0:T(8,128)(2,1)S(1)}, u32[]{:S(2)}, u32[]{:S(2)}) collective-permute-start(bf16[48,1664]{1,0:T(8,128)(2,1)} %get-tuple-element.131), channel_id=1, source_target_pairs={{0,8},{1,9},{2,10},{3,11},{4,12},{5,13},{6,14},{7,15},{8,0},{9,1},... | collective-permute-start | bytes 479240 | tf_op jit(solution)/shard_map/ppermute | solution.py:46
  17.3 23.3 %collective-permute-start.2 = (bf16[48,1664]{1,0:T(8,128)(2,1)}, bf16[48,1664]{1,0:T(8,128)(2,1)S(1)}, u32[]{:S(2)}, u32[]{:S(2)}) collective-permute-start(bf16[48,1664]{1,0:T(8,128)(2,1)} %get-tuple-element.131), channel_id=1, source_target_pairs={{0,12},{1,13},{2,14},{3,15},{4,8},{5,9},{6,10},{7,11},{8,4},{9,5},... | collective-permute-start | bytes 479240 | tf_op jit(solution)/shard_map/ppermute | solution.py:46
  19.5 45.1 %collective-permute-start.7 = (bf16[48,1536]{1,0:T(8,128)(2,1)S(1)}, bf16[48,1536]{1,0:T(8,128)(2,1)S(1)}, u32[]{:S(2)}, u32[]{:S(2)}) collective-permute-start(bf16[48,1536]{1,0:T(8,128)(2,1)S(1)} %get-tuple-element.97), channel_id=1, source_target_pairs={{0,4},{1,5},{2,6},{3,7},{4,0},{5,1},{6,2},{7,3},{8,12},{9,13},{10,... | collective-permute-start | bytes 442376 | tf_op jit(solution)/shard_map/ppermute | solution.py:46
  19.5 45.1 %collective-permute-start.8 = (bf16[48,1536]{1,0:T(8,128)(2,1)S(1)}, bf16[48,1536]{1,0:T(8,128)(2,1)S(1)}, u32[]{:S(2)}, u32[]{:S(2)}) collective-permute-start(bf16[48,1536]{1,0:T(8,128)(2,1)S(1)} %get-tuple-element.97), channel_id=1, source_target_pairs={{0,8},{1,9},{2,10},{3,11},{4,12},{5,13},{6,14},{7,15},{8,0},{9,1},... | collective-permute-start | bytes 442376 | tf_op jit(solution)/shard_map/ppermute | solution.py:46
  31.8 32.8 %collective-permute-start.9 = (bf16[48,1536]{1,0:T(8,128)(2,1)S(1)}, bf16[48,1536]{1,0:T(8,128)(2,1)S(1)}, u32[]{:S(2)}, u32[]{:S(2)}) collective-permute-start(bf16[48,1536]{1,0:T(8,128)(2,1)S(1)} %get-tuple-element.97), channel_id=1, source_target_pairs={{0,12},{1,13},{2,14},{3,15},{4,8},{5,9},{6,10},{7,11},{8,4},{9,5},... | collective-permute-start | bytes 442376 | tf_op jit(solution)/shard_map/ppermute | solution.py:46
  39.1 41.5 %collective-permute-start.16 = (bf16[768,384]{1,0:T(8,128)(2,1)S(1)}, bf16[768,384]{1,0:T(8,128)(2,1)S(1)}, u32[]{:S(2)}, u32[]{:S(2)}) collective-permute-start(bf16[768,384]{1,0:T(8,128)(2,1)S(1)} %pad_maximum_fusion.3), channel_id=1, source_target_pairs={{0,1},{1,0},{2,3},{3,2},{4,5},{5,4},{6,7},{7,6},{8,9},{9,8},{10,11... | collective-permute-start | bytes 1769480 | tf_op jit(solution)/shard_map/ppermute | solution.py:46
  40.7 22.2 %collective-permute-start.3 = (bf16[192,1664]{1,0:T(8,128)(2,1)S(1)}, bf16[192,1664]{1,0:T(8,128)(2,1)S(1)}, u32[]{:S(2)}, u32[]{:S(2)}) collective-permute-start(bf16[192,1664]{1,0:T(8,128)(2,1)S(1)} %pad_maximum_fusion.1), channel_id=1, source_target_pairs={{0,1},{1,0},{2,3},{3,2},{4,5},{5,4},{6,7},{7,6},{8,9},{9,8},{10,11... | collective-permute-start | bytes 1916936 | tf_op jit(solution)/shard_map/ppermute | solution.py:46
  63.0 17.3 %collective-permute-start.4 = (bf16[384,1664]{1,0:T(8,128)(2,1)S(1)}, bf16[384,1664]{1,0:T(8,128)(2,1)S(1)}, u32[]{:S(2)}, u32[]{:S(2)}) collective-permute-start(bf16[384,1664]{1,0:T(8,128)(2,1)S(1)} %get-tuple-element.109), channel_id=1, source_target_pairs={{0,2},{1,3},{2,0},{3,1},{4,6},{5,7},{6,4},{7,5},{8,10},{9,11},{10,... | collective-permute-start | bytes 3833864 | tf_op jit(solution)/shard_map/ppermute | solution.py:46
  64.7 18.6 %collective-permute-start.10 = (bf16[192,1536]{1,0:T(8,128)(2,1)S(1)}, bf16[192,1536]{1,0:T(8,128)(2,1)S(1)}, u32[]{:S(2)}, u32[]{:S(2)}) collective-permute-start(bf16[192,1536]{1,0:T(8,128)(2,1)S(1)} %pad_maximum_fusion.2), channel_id=1, source_target_pairs={{0,1},{1,0},{2,3},{3,2},{4,5},{5,4},{6,7},{7,6},{8,9},{9,8},{10,11... | collective-permute-start | bytes 1769480 | tf_op jit(solution)/shard_map/ppermute | solution.py:46
  80.5 32.5 %collective-permute-start.5 = (bf16[768,1664]{1,0:T(8,128)(2,1)S(1)}, bf16[768,1664]{1,0:T(8,128)(2,1)}, u32[]{:S(2)}, u32[]{:S(2)}) collective-permute-start(bf16[768,1664]{1,0:T(8,128)(2,1)S(1)} %constant_dynamic-update-slice_fusion.5.mine_ref.mine), channel_id=1, source_target_pairs={{0,16},{16,0},{1,17},{17,1},{2,18},{18,2},{3,19},{19,3},{4,20},{20... | collective-permute-start | bytes 7667720 | tf_op jit(solution)/shard_map/ppermute | solution.py:39
  81.8 16.2 %collective-permute-start.17 = (bf16[1536,384]{1,0:T(8,128)(2,1)S(1)}, bf16[1536,384]{1,0:T(8,128)(2,1)S(1)}, u32[]{:S(2)}, u32[]{:S(2)}) collective-permute-start(bf16[1536,384]{1,0:T(8,128)(2,1)S(1)} %get-tuple-element.111), channel_id=1, source_target_pairs={{0,2},{1,3},{2,0},{3,1},{4,6},{5,7},{6,4},{7,5},{8,10},{9,11},{10,... | collective-permute-start | bytes 3538952 | tf_op jit(solution)/shard_map/ppermute | solution.py:46
  84.2 26.4 %collective-permute-start.11 = (bf16[384,1536]{1,0:T(8,128)(2,1)S(1)}, bf16[384,1536]{1,0:T(8,128)(2,1)S(1)}, u32[]{:S(2)}, u32[]{:S(2)}) collective-permute-start(bf16[384,1536]{1,0:T(8,128)(2,1)S(1)} %get-tuple-element.113), channel_id=1, source_target_pairs={{0,2},{1,3},{2,0},{3,1},{4,6},{5,7},{6,4},{7,5},{8,10},{9,11},{10,... | collective-permute-start | bytes 3538952 | tf_op jit(solution)/shard_map/ppermute | solution.py:46
  99.1 53.3 %collective-permute-start.18 = (bf16[3072,384]{1,0:T(8,128)(2,1)}, bf16[3072,384]{1,0:T(8,128)(2,1)}, u32[]{:S(2)}, u32[]{:S(2)}) collective-permute-start(bf16[3072,384]{1,0:T(8,128)(2,1)} %constant_dynamic-update-slice_fusion.27.dm), channel_id=1, source_target_pairs={{0,16},{16,0},{1,17},{17,1},{2,18},{18,2},{3,19},{19,3},{4,20},{20... | collective-permute-start | bytes 7077896 | tf_op jit(solution)/shard_map/ppermute | solution.py:39
  111.7 40.7 %collective-permute-start.12 = (bf16[768,1536]{1,0:T(8,128)(2,1)}, bf16[768,1536]{1,0:T(8,128)(2,1)}, u32[]{:S(2)}, u32[]{:S(2)}) collective-permute-start(bf16[768,1536]{1,0:T(8,128)(2,1)} %constant_dynamic-update-slice_fusion.16.um), channel_id=1, source_target_pairs={{0,16},{16,0},{1,17},{17,1},{2,18},{18,2},{3,19},{19,3},{4,20},{20... | collective-permute-start | bytes 7077896 | tf_op jit(solution)/shard_map/ppermute | solution.py:39
  178.5 57.8 %collective-permute-start.34 = (bf16[3072,384]{1,0:T(8,128)(2,1)}, bf16[3072,384]{1,0:T(8,128)(2,1)}, u32[]{:S(2)}, u32[]{:S(2)}) collective-permute-start(bf16[3072,384]{1,0:T(8,128)(2,1)} %get-tuple-element.85), channel_id=1, source_target_pairs={{0,16},{16,0},{1,17},{17,1},{2,18},{18,2},{3,19},{19,3},{4,20},{20... | collective-permute-start | bytes 7077896 | tf_op jit(solution)/shard_map/ppermute | solution.py:39
  221.4 18.1 %collective-permute-start.27 = (bf16[768,1536]{1,0:T(8,128)(2,1)}, bf16[768,1536]{1,0:T(8,128)(2,1)}, u32[]{:S(2)}, u32[]{:S(2)}) collective-permute-start(bf16[768,1536]{1,0:T(8,128)(2,1)} %get-tuple-element.83), channel_id=1, source_target_pairs={{0,16},{16,0},{1,17},{17,1},{2,18},{18,2},{3,19},{19,3},{4,20},{20... | collective-permute-start | bytes 7077896 | tf_op jit(solution)/shard_map/ppermute | solution.py:39
  236.1 41.3 %collective-permute-start.20 = (bf16[768,1664]{1,0:T(8,128)(2,1)}, bf16[768,1664]{1,0:T(8,128)(2,1)S(1)}, u32[]{:S(2)}, u32[]{:S(2)}) collective-permute-start(bf16[768,1664]{1,0:T(8,128)(2,1)} %get-tuple-element.81), channel_id=1, source_target_pairs={{0,16},{16,0},{1,17},{17,1},{2,18},{18,2},{3,19},{19,3},{4,20},{20... | collective-permute-start | bytes 7667720 | tf_op jit(solution)/shard_map/ppermute | solution.py:39
  238.0 16.3 %collective-permute-start.35 = (bf16[1536,384]{1,0:T(8,128)(2,1)S(1)}, bf16[1536,384]{1,0:T(8,128)(2,1)S(1)}, u32[]{:S(2)}, u32[]{:S(2)}) collective-permute-start(bf16[1536,384]{1,0:T(8,128)(2,1)S(1)} %reduce-precision_convert_fusion.1), channel_id=1, source_target_pairs={{0,2},{1,3},{2,0},{3,1},{4,6},{5,7},{6,4},{7,5},{8,10},{9,11},{10,... | collective-permute-start | bytes 3538952 | tf_op jit(solution)/shard_map/ppermute | solution.py:46
  241.1 32.2 %collective-permute-start.28 = (bf16[384,1536]{1,0:T(8,128)(2,1)S(1)}, bf16[384,1536]{1,0:T(8,128)(2,1)S(1)}, u32[]{:S(2)}, u32[]{:S(2)}) collective-permute-start(bf16[384,1536]{1,0:T(8,128)(2,1)S(1)} %reduce-precision_convert_fusion.2), channel_id=1, source_target_pairs={{0,2},{1,3},{2,0},{3,1},{4,6},{5,7},{6,4},{7,5},{8,10},{9,11},{10,... | collective-permute-start | bytes 3538952 | tf_op jit(solution)/shard_map/ppermute | solution.py:46
  256.9 41.3 %collective-permute-start.36 = (bf16[768,384]{1,0:T(8,128)(2,1)}, bf16[768,384]{1,0:T(8,128)(2,1)S(1)}, u32[]{:S(2)}, u32[]{:S(2)}) collective-permute-start(bf16[768,384]{1,0:T(8,128)(2,1)} %reduce-precision_convert_fusion.4), channel_id=1, source_target_pairs={{0,1},{1,0},{2,3},{3,2},{4,5},{5,4},{6,7},{7,6},{8,9},{9,8},{10,11... | collective-permute-start | bytes 1769480 | tf_op jit(solution)/shard_map/ppermute | solution.py:46
  275.8 16.2 %collective-permute-start.29 = (bf16[192,1536]{1,0:T(8,128)(2,1)}, bf16[192,1536]{1,0:T(8,128)(2,1)}, u32[]{:S(2)}, u32[]{:S(2)}) collective-permute-start(bf16[192,1536]{1,0:T(8,128)(2,1)} %reduce-precision_convert_fusion.5), channel_id=1, source_target_pairs={{0,1},{1,0},{2,3},{3,2},{4,5},{5,4},{6,7},{7,6},{8,9},{9,8},{10,11... | collective-permute-start | bytes 1769480 | tf_op jit(solution)/shard_map/ppermute | solution.py:46
  278.8 33.1 %collective-permute-start.21 = (bf16[384,1664]{1,0:T(8,128)(2,1)}, bf16[384,1664]{1,0:T(8,128)(2,1)}, u32[]{:S(2)}, u32[]{:S(2)}) collective-permute-start(bf16[384,1664]{1,0:T(8,128)(2,1)} %reduce-precision_convert_fusion), channel_id=1, source_target_pairs={{0,2},{1,3},{2,0},{3,1},{4,6},{5,7},{6,4},{7,5},{8,10},{9,11},{10,... | collective-permute-start | bytes 3833864 | tf_op jit(solution)/shard_map/ppermute | solution.py:46
  317.5 25.4 %collective-permute-start.40 = (bf16[192,384]{1,0:T(8,128)(2,1)S(1)}, bf16[192,384]{1,0:T(8,128)(2,1)S(1)}, u32[]{:S(2)}, u32[]{:S(2)}) collective-permute-start(bf16[192,384]{1,0:T(8,128)(2,1)S(1)} %reduce-precision_convert_fusion.10), channel_id=1, source_target_pairs={{0,16},{16,0},{1,17},{17,1},{2,18},{18,2},{3,19},{19,3},{4,20},{20... | collective-permute-start | bytes 442376 | tf_op jit(solution)/shard_map/ppermute | solution.py:39
  (33 other events, 335.5 us)
